TPU v7x, 32 devices: a whole 2x2x4 slice. The times are simulated.
32 devices in a mesh: ctx: 8 (over z, y), pack: 4 (over x, core).
Axes of the slice: x: 2, y: 2, z: 4, core: 2. Of those that a mesh axis runs over, the one named last changes fastest.
Arguments:
- hidden: bfloat16 [8192, 2048], P(('ctx', 'pack')), may hold values from -4 to 4
- first_keys: bfloat16 [8192, 2048], P('ctx', 'pack'), may hold values from -400 to 400
- first_values: bfloat16 [8192, 2048], P('ctx', 'pack'), may hold values from -18 to 18
- w_query: bfloat16 [2048, 2048], P(None, 'pack'), may hold values from -0.125 to 0.125
- w_out: bfloat16 [2048, 2048], P('pack'), may hold values from -0.125 to 0.125
- norm_gain: float32 [2048], replicated, may hold values from 0.1 to 1.9
- router_weight: float32 [2048], replicated, may hold values from -0.5 to 0.5
- route_list: int32 [8, 256], P('ctx'), may hold values from 0 to 1023, as said below
- pack_order: int32 [8, 256], P('ctx'), may hold values from 0 to 255, each once within a row
- pattern: int32 [8, 12], replicated, may hold values from 0 to 7
Outputs:
- hidden_out: bfloat16 [8192, 2048], P(('ctx', 'pack'))
- packed_states: bfloat16 [2048, 2048], P(('ctx', 'pack'))
Inputs may be any that keep to these rules, and one draw needn't show every extreme that they name: `route_list`: each row lists 256 distinct span-local positions in ascending order. At most 96 of a row's positions lie among the 256 tokens of one device, and in every row some device holds exactly 96.
All inputs are finite; a program needn't handle non-finite values.
Results may differ from a plain program's by a relative error of at most 0.023.
Values may be sent and summed in bfloat16 or wider, within the bound.
No kernel may reach another device: no remote copies, remote signals or barrier semaphores. Data moves between devices by JAX's collectives and lax.ppermute only.
A program may use at most 128 MiB of HBM per device.

v0:
```python
import functools
import math

import jax
import jax.numpy as jnp
from jax import lax
from jax.experimental import pallas as pl
from jax.experimental.pallas import tpu as pltpu
from jax.sharding import PartitionSpec as P


HD = 128
EPS = 1e-06
NEG = -1e30
TAIL = 32
SCALE = math.log2(math.e) / math.sqrt(HD)


def contract(left, right, left_dim, right_dim):
    return lax.dot_general(
        left, right, (((left_dim,), (right_dim,)), ((), ())), preferred_element_type=jnp.float32
    )


def run(body, *, grid, scalars, in_specs, out_specs, out_shape, scratch=(), cost=None, mib=16):
    kernel = call(body, grid, scalars, in_specs, out_specs, out_shape, scratch, cost, mib)

    return kernel


def call(body, grid, scalars, in_specs, out_specs, out_shape, scratch, cost, mib):
    return pl.pallas_call(
        body,
        grid_spec=pltpu.PrefetchScalarGridSpec(
            num_scalar_prefetch=scalars,
            grid=grid,
            in_specs=in_specs,
            out_specs=out_specs,
            scratch_shapes=list(scratch),
        ),
        out_shape=out_shape,
        cost_estimate=cost,
        compiler_params=pltpu.CompilerParams(vmem_limit_bytes=mib * 2**20),
    )


def cost_of(flops, moved, exps=0):
    return pl.CostEstimate(flops=int(flops), bytes_accessed=int(moved), transcendentals=int(exps))


def below(routes, bound):
    return jnp.sum(jnp.where(routes < bound, 1.0, 0.0), axis=1, keepdims=True).astype(jnp.int32)


def pick_body(ids, routes_ref, hidden_ref, out_ref):
    tok = hidden_ref.shape[0]
    cap = out_ref.shape[0]
    routed = routes_ref.shape[1]
    base = ids[1] * tok
    routes = routes_ref[...]
    token = lax.broadcasted_iota(jnp.int32, (tok, routed), 0) + base
    hit = jnp.where(routes == token, 1.0, 0.0).astype(jnp.bfloat16)
    entry = lax.broadcasted_iota(jnp.int32, (cap, routed), 1)
    slot = lax.broadcasted_iota(jnp.int32, (cap, routed), 0)
    choose = jnp.where(entry == slot + below(routes, base), 1.0, 0.0).astype(jnp.bfloat16)
    one_hot = contract(choose, hit, 1, 1).astype(jnp.bfloat16)
    out_ref[...] = contract(one_hot, hidden_ref[...], 1, 0).astype(out_ref.dtype)


def query_body(xors, tok, ids, *refs):
    count = len(xors)
    pieces = refs[:count]
    routes_ref, order_ref, gain_ref, router_ref, cos_ref, sin_ref, wq_ref = refs[count : count + 7]
    rows_ref, gate_ref, query_ref = refs[count + 7 :]
    cap = pieces[0].shape[0]
    routed = order_ref.shape[1]
    routes = routes_ref[...]
    order = order_ref[...]
    entry = lax.broadcasted_iota(jnp.int32, (cap, routed), 0)
    rows = None
    for xor, piece in zip(xors, pieces):
        owner = ids[1] ^ xor
        listed = entry + below(routes, owner * tok)
        stop = below(routes, (owner + 1) * tok)
        one_hot = jnp.where((order == listed) & (listed < stop), 1.0, 0.0).astype(jnp.bfloat16)
        term = contract(one_hot, piece[...], 0, 0)
        rows = term if rows is None else rows + term
    rows_ref[...] = rows.astype(rows_ref.dtype)
    logit = jnp.sum(rows * router_ref[...], axis=1, keepdims=True)
    gate_ref[...] = jnp.broadcast_to(1.0 / (1.0 + jnp.exp(-logit)), gate_ref.shape)
    mean_square = jnp.mean(rows * rows, axis=1, keepdims=True)
    normed = (rows * lax.rsqrt(mean_square + EPS) * gain_ref[...]).astype(jnp.bfloat16)
    projected = contract(normed, wq_ref[...], 1, 0)
    cosine = cos_ref[...]
    sine = sin_ref[...]
    for head in range(query_ref.shape[1] // HD):
        part = projected[:, head * HD : (head + 1) * HD]
        turned = part * cosine + pltpu.roll(part, HD // 2, 1) * sine
        query_ref[:, head * HD : (head + 1) * HD] = turned.astype(query_ref.dtype)


def attend_body(shift, use, n_ctx, chunk, ids, pattern, *refs):
    masked_own = shift == 0 and "own" in use
    if masked_own:
        qpos_ref, refs = refs[0], refs[1:]
    q_ref, refs = refs[0], refs[1:]
    spans = [(refs[2 * i], refs[2 * i + 1]) for i in range(len(use))]
    out_ref, m_ref, l_ref, acc_ref, log_ref = refs[2 * len(use) :]
    head = pl.program_id(1)
    span = spans[0][0].shape[0]
    width = out_ref.shape[0] - TAIL
    here = ids[0]
    source = here + 2 * shift
    row = jnp.minimum(source, n_ctx - 1)

    def attends(key_span):
        found = pattern[row, 0] == key_span
        for at in range(1, pattern.shape[1]):
            found = found | (pattern[row, at] == key_span)
        return found & (source < n_ctx) & (key_span < source)

    m_ref[...] = jnp.full_like(m_ref, NEG)
    l_ref[...] = jnp.zeros_like(l_ref)
    acc_ref[...] = jnp.zeros_like(acc_ref)

    def block(k_ref, v_ref, masked):
        for at in range(0, span, chunk):
            scores = contract(k_ref[at : at + chunk, :], q_ref[...], 1, 1) * SCALE
            if masked:
                kpos = lax.broadcasted_iota(jnp.int32, scores.shape, 0) + at
                scores = jnp.where(kpos <= qpos_ref[...], scores, NEG)
            former = m_ref[...]
            peak = jnp.maximum(former, jnp.max(scores, axis=0, keepdims=True))
            weights = jnp.exp2(scores - peak)
            fade = jnp.exp2(former - peak)
            m_ref[...] = peak
            l_ref[...] = l_ref[...] * fade + jnp.sum(weights, axis=0, keepdims=True)
            acc_ref[...] = acc_ref[...] * fade + contract(
                v_ref[at : at + chunk, :], weights.astype(jnp.bfloat16), 0, 0
            )

    for kind, (k_ref, v_ref) in zip(use, spans):
        if kind == "own" and shift == 0:
            block(k_ref, v_ref, True)
        else:
            key_span = here if kind == "own" else here ^ 1
            pl.when(attends(key_span))(functools.partial(block, k_ref, v_ref, False))

    total = l_ref[...]
    some = total > 0.0
    safe = jnp.where(some, total, 1.0)
    out_ref[pl.ds(pl.multiple_of(head * HD, HD), HD), :] = (acc_ref[...] / safe).astype(
        out_ref.dtype
    )
    log_ref[pl.ds(head, 1), :] = jnp.where(some, m_ref[...] + jnp.log2(safe), NEG)

    @pl.when(head == pl.num_programs(1) - 1)
    def _():
        level = log_ref[...]
        high = level.astype(jnp.bfloat16).astype(jnp.float32)
        rest = level - high
        middle = rest.astype(jnp.bfloat16).astype(jnp.float32)
        low = rest - middle
        out_ref[width:, :] = jnp.concatenate(
            [high, middle, low, jnp.zeros_like(low)], axis=0
        ).astype(out_ref.dtype)


def merge_body(shifts, ids, *refs):
    parts, out_ref = refs[:-1], refs[-1]
    width = out_ref.shape[0]
    levels = []
    for shift, part in zip(shifts, parts):
        tail = part[width:, :].astype(jnp.float32)
        level = tail[0:8] + tail[8:16] + tail[16:24]
        if shift:
            level = jnp.where(ids[0] >= 2 * shift, level, NEG)
        levels.append(level)
    peak = functools.reduce(jnp.maximum, levels)
    weights = [jnp.exp2(level - peak) for level in levels]
    inverse = 1.0 / functools.reduce(lambda a, b: a + b, weights)
    for head in range(width // HD):
        cut = slice(head * HD, (head + 1) * HD)
        total = None
        for weight, part in zip(weights, parts):
            term = part[cut, :].astype(jnp.float32) * (weight * inverse)[head : head + 1, :]
            total = term if total is None else total + term
        out_ref[cut, :] = total.astype(out_ref.dtype)


def finish_body(count, ids, *refs):
    attended = refs[:count]
    weights = refs[count : 2 * count]
    rows_ref, gate_ref, picked_ref, hidden_ref = refs[2 * count : 2 * count + 4]
    hidden_out, packed_out, flat_ref, place_ref, new_ref = refs[2 * count + 4 :]
    tok = hidden_ref.shape[0]
    routed = rows_ref.shape[0]
    own = packed_out.shape[0]
    part = attended[0].shape[0]

    @pl.when(pl.program_id(0) == 0)
    def _():
        for at in range(count):
            flat_ref[:, at * part : (at + 1) * part] = jnp.transpose(attended[at][...])
        token = lax.broadcasted_iota(jnp.int32, (tok, routed), 0) + ids[1] * tok
        place_ref[...] = jnp.where(picked_ref[...] == token, 1.0, 0.0).astype(place_ref.dtype)

    mixed = None
    for at in range(count):
        term = contract(flat_ref[:, at * part : (at + 1) * part], weights[at][...], 1, 0)
        mixed = term if mixed is None else mixed + term
    new = rows_ref[...].astype(jnp.float32) + gate_ref[:, 0:1] * mixed
    new_ref[...] = new.astype(new_ref.dtype)
    packed_out[...] = new_ref[pl.ds(pl.multiple_of(ids[1] * own, own), own), :]
    place = place_ref[...]
    moved = contract(place, new_ref[...], 1, 0)
    filled = jnp.sum(place.astype(jnp.float32), axis=1, keepdims=True) > 0.0
    hidden_out[...] = jnp.where(filled, moved, hidden_ref[...].astype(jnp.float32)).astype(
        hidden_out.dtype
    )


def gather_pack(piece, n_pack):
    pieces, xors = [piece], [0]
    bit = n_pack // 2
    while bit:
        pairs = [(p, p ^ bit) for p in range(n_pack)]
        pieces = pieces + [lax.ppermute(held, "pack", pairs) for held in pieces]
        xors = xors + [x ^ bit for x in xors]
        bit //= 2
    return pieces, xors


def local(
    hidden,
    first_keys,
    first_values,
    w_query,
    w_out,
    norm_gain,
    router_weight,
    route_list,
    pack_order,
    pattern,
):
    n_ctx = lax.axis_size("ctx")
    n_pack = lax.axis_size("pack")
    ctx = lax.axis_index("ctx")
    pack = lax.axis_index("pack")
    tok, width = hidden.shape
    span, part = first_keys.shape
    heads = part // HD
    routed = route_list.shape[1]
    own = routed // n_pack
    cap = 3 * tok // 8
    ids = jnp.stack([ctx, pack]).astype(jnp.int32)
    whole = lambda shape: pl.BlockSpec(shape, lambda *_: (0,) * len(shape))
    bf16, f32 = jnp.bfloat16, jnp.float32

    outgoing = run(
        pick_body,
        grid=(1,),
        scalars=1,
        in_specs=[whole((1, routed)), whole((tok, width))],
        out_specs=whole((cap, width)),
        out_shape=jax.ShapeDtypeStruct((cap, width), bf16),
        cost=cost_of(2 * cap * tok * width, 2 * tok * width * 2),
    )(ids, route_list, hidden)

    pieces, xors = gather_pack(outgoing, n_pack)

    swap = [(c, c ^ 1) for c in range(n_ctx)]
    keys_in, values_in, _ = lax.optimization_barrier((first_keys, first_values, outgoing))
    other_keys = lax.ppermute(keys_in, "ctx", swap)
    other_values = lax.ppermute(values_in, "ctx", swap)

    picked = jnp.sum(
        jnp.where(
            pack_order[0][:, None] == jnp.arange(routed, dtype=jnp.int32)[None, :],
            route_list[0][None, :],
            0,
        ),
        axis=1,
    )
    position = picked + ctx * span
    half = HD // 2
    frequency = 10000.0 ** (-jnp.arange(half, dtype=f32) * 2.0 / HD)
    angle = position.astype(f32)[:, None] * frequency[None, :]
    cosine, sine = jnp.cos(angle), jnp.sin(angle)
    cosine = jnp.concatenate([cosine, cosine], axis=1)
    sine = jnp.concatenate([-sine, sine], axis=1)

    rows, gate, queries = run(
        functools.partial(query_body, xors, tok),
        grid=(1,),
        scalars=1,
        in_specs=[whole((cap, width))] * n_pack
        + [
            whole((1, routed)),
            whole((1, routed)),
            whole((1, width)),
            whole((1, width)),
            whole((routed, HD)),
            whole((routed, HD)),
            whole((width, part)),
        ],
        out_specs=[whole((routed, width)), whole((routed, HD)), whole((routed, part))],
        out_shape=[
            jax.ShapeDtypeStruct((routed, width), bf16),
            jax.ShapeDtypeStruct((routed, HD), f32),
            jax.ShapeDtypeStruct((routed, part), bf16),
        ],
        cost=cost_of(2 * routed * width * (part + n_pack * cap), 6 * width * part),
        mib=32,
    )(
        ids,
        *pieces,
        route_list,
        pack_order,
        norm_gain.reshape(1, width),
        router_weight.reshape(1, width),
        cosine,
        sine,
        w_query,
    )

    w_in, _ = lax.optimization_barrier((w_out, pieces[1]))
    w_pieces, _ = gather_pack(w_in, n_pack)

    q_block = min(routed, 256)
    chunk = min(span, 1024)
    tall = part + TAIL
    pair_flops = 4 * routed * span * part

    def attend(shift, query, use):
        masked = shift == 0 and "own" in use
        extra = [pl.BlockSpec((1, q_block), lambda i, h, *_: (0, i))] if masked else []
        given = [picked.reshape(1, routed)] if masked else []
        column = lambda i, h, *_: (0, h)
        held = {"own": (first_keys, first_values), "other": (other_keys, other_values)}
        arrays = [array for kind in use for array in held[kind]]
        return run(
            functools.partial(attend_body, shift, use, n_ctx, chunk),
            grid=(routed // q_block, heads),
            scalars=2,
            in_specs=extra
            + [pl.BlockSpec((q_block, HD), lambda i, h, *_: (i, h))]
            + [pl.BlockSpec((span, HD), column)] * len(arrays),
            out_specs=pl.BlockSpec((tall, q_block), lambda i, h, *_: (0, i)),
            out_shape=jax.ShapeDtypeStruct((tall, routed), bf16),
            scratch=[
                pltpu.VMEM((1, q_block), f32),
                pltpu.VMEM((1, q_block), f32),
                pltpu.VMEM((HD, q_block), f32),
                pltpu.VMEM((8, q_block), f32),
            ],
            cost=cost_of(len(use) * pair_flops, 4 * span * part * len(use)),
        )(ids, pattern, *given, query, *arrays)

    far = n_ctx // 2 - 1
    moved = {}
    for shift in range(far, 0, -1):
        moved[shift] = lax.ppermute(
            queries, "ctx", [(c, c - 2 * shift) for c in range(2 * shift, n_ctx)]
        )
    parts = [attend(0, queries, ("own",))]
    for shift in range(far, 0, -1):
        partial = attend(shift, moved[shift], ("own", "other"))
        parts.append(
            lax.ppermute(partial, "ctx", [(c, c + 2 * shift) for c in range(n_ctx - 2 * shift)])
        )
    parts.append(attend(0, queries, ("other",)))
    shifts = [0, *range(far, 0, -1), 0]

    attended = run(
        functools.partial(merge_body, shifts),
        grid=(1,),
        scalars=1,
        in_specs=[whole((tall, routed))] * len(parts),
        out_specs=whole((part, routed)),
        out_shape=jax.ShapeDtypeStruct((part, routed), bf16),
        cost=cost_of(8 * routed * part, 2 * tall * routed * len(parts)),
    )(ids, *parts)

    a_pieces, _ = gather_pack(attended, n_pack)

    columns = width // 4
    slab = lambda rows_: pl.BlockSpec((rows_, columns), lambda j, *_: (0, j))
    hidden_out, packed = run(
        functools.partial(finish_body, n_pack),
        grid=(width // columns,),
        scalars=1,
        in_specs=[whole((part, routed))] * n_pack
        + [slab(part)] * n_pack
        + [slab(routed), whole((routed, HD)), whole((1, routed)), slab(tok)],
        out_specs=[slab(tok), slab(own)],
        out_shape=[
            jax.ShapeDtypeStruct((tok, width), hidden.dtype),
            jax.ShapeDtypeStruct((own, width), hidden.dtype),
        ],
        scratch=[
            pltpu.VMEM((routed, n_pack * part), bf16),
            pltpu.VMEM((tok, routed), bf16),
            pltpu.VMEM((routed, columns), bf16),
        ],
        cost=cost_of(2 * routed * width * width, 2 * width * width),
        mib=24,
    )(ids, *a_pieces, *w_pieces, rows, gate, picked.reshape(1, routed), hidden)
    return (hidden_out, packed)


def solution(mesh):
    return jax.shard_map(
        local,
        mesh=mesh,
        in_specs=(
            P(("ctx", "pack"), None),
            P("ctx", "pack"),
            P("ctx", "pack"),
            P(None, "pack"),
            P("pack", None),
            P(),
            P(),
            P("ctx", None),
            P("ctx", None),
            P(),
        ),
        out_specs=(P(("ctx", "pack"), None), P(("ctx", "pack"), None)),
        check_vma=False,
    )
```

profile of v0, /device:TPU:7, one launch (start us, length us, event | category | flops | bytes accessed | tf_op | source)
XLA Modules:
  0.0 138.3 jit_solution(1338632882360297584)
XLA Ops:
  0.6 0.0 copy-start.8
  0.7 0.1 pad_add_fusion.ids
  0.7 1.2 copy-done.2
  2.0 0.7 copy-done.7
  2.6 1.0 shard_map.113.refs_0_
  3.7 0.3 collective-permute-start
  4.0 9.7 %collective-permute-done.refs_1_ = bf16[96,2048]{1,0:T(8,128)(2,1)S(1)} collective-permute-done((bf16[96,2048]{1,0:T(8,128)(2,1)S(1)}, bf16[96,2048]{1,0:T(8,128)(2,1)S(1)}, u32[]{:S(2)}, u32[]{:S(2)}) %collective-permute-start) | collective-permute-done | bytes 393248 | tf_op jit(solution)/shard_map/ppermute | solution.py:228
  13.8 0.3 collective-permute-start.14
  14.0 1.8 %collective-permute-start.1 = (bf16[96,2048]{1,0:T(8,128)(2,1)S(1)}, bf16[96,2048]{1,0:T(8,128)(2,1)S(1)}, u32[]{:S(2)}, u32[]{:S(2)}) collective-permute-start(bf16[96,2048]{1,0:T(8,128)(2,1)S(1)} %shard_map.113.refs_0_), channel_id=1, source_target_pairs={{0,1},{1,0},{2,3},{3,2},{4,5},{5,4},{6,7},{7,6},{8,9},{9,8},{10,11... | collective-permute-start | bytes 1179656 | tf_op jit(solution)/shard_map/ppermute | solution.py:228
  15.8 0.0 collective-permute-start.4
  15.8 1.5 %collective-permute-start.5 = (bf16[1024,512]{1,0:T(8,128)(2,1)}, bf16[1024,512]{1,0:T(8,128)(2,1)S(1)}, u32[]{:S(2)}, u32[]{:S(2)}) collective-permute-start(bf16[1024,512]{1,0:T(8,128)(2,1)} %refs_2_.7), channel_id=1, source_target_pairs={{0,4},{4,0},{8,12},{12,8},{16,20},{20,16},{24,28},{28,24},{1,5},{5... | collective-permute-start | bytes 3145736 | tf_op jit(solution)/shard_map/ppermute | solution.py:275
  17.3 0.9 select_reduce_fusion
  18.2 0.6 collective-permute-start.15
  18.8 40.9 %collective-permute-done.14.refs_5_ = bf16[512,2048]{1,0:T(8,128)(2,1)} collective-permute-done((bf16[512,2048]{1,0:T(8,128)(2,1)}, bf16[512,2048]{1,0:T(8,128)(2,1)}, u32[]{:S(2)}, u32[]{:S(2)}) %collective-permute-start.14) | collective-permute-done | bytes 2097184 | tf_op jit(solution)/shard_map/ppermute | solution.py:228
  59.7 2.4 %collective-permute-start.16 = (bf16[512,2048]{1,0:T(8,128)(2,1)}, bf16[512,2048]{1,0:T(8,128)(2,1)S(1)}, u32[]{:S(2)}, u32[]{:S(2)}) collective-permute-start(bf16[512,2048]{1,0:T(8,128)(2,1)} %collective-permute-done.14.refs_5_), channel_id=1, source_target_pairs={{0,1},{1,0},{2,3},{3,2},{4,5},{5,4},{6,7},{7,6},{8,9},{9,8},{10,11... | collective-permute-start | bytes 6291464 | tf_op jit(solution)/shard_map/ppermute | solution.py:228
  62.1 0.0 collective-permute-done.1.refs_2_
  62.1 0.1 collective-permute-start.2
  62.2 0.5 fusion
  62.8 0.0 copy-start.6
  62.8 0.1 pad_maximum_fusion
  62.9 0.0 copy-start
  62.9 0.0 copy-start.1
  62.9 3.7 %collective-permute-done.2.refs_3_ = bf16[96,2048]{1,0:T(8,128)(2,1)S(1)} collective-permute-done((bf16[96,2048]{1,0:T(8,128)(2,1)S(1)}, bf16[96,2048]{1,0:T(8,128)(2,1)S(1)}, u32[]{:S(2)}, u32[]{:S(2)}) %collective-permute-start.2) | collective-permute-done | bytes 393248 | tf_op jit(solution)/shard_map/ppermute | solution.py:228
  66.7 0.0 copy-start.4
  66.7 1.6 %copy-done.4 = bf16[2048,512]{1,0:T(8,128)(2,1)S(1)} copy-done((bf16[2048,512]{1,0:T(8,128)(2,1)S(1)}, bf16[2048,512]{1,0:T(8,128)(2,1)}, u32[]{:S(2)}) %copy-start.4) | copy-done | bytes 2097176
  68.3 2.9 %shard_map.114 = (bf16[256,2048]{1,0:T(8,128)(2,1)S(1)}, f32[256,128]{1,0:T(8,128)S(1)}, bf16[256,512]{1,0:T(8,128)(2,1)S(1)}) custom-call(s32[2]{0:T(128)S(1)} %pad_add_fusion.ids, bf16[96,2048]{1,0:T(8,128)(2,1)S(1)} %shard_map.113.refs_0_, bf16[96,2048]{1,0:T(8,128)(2,1)S(1)} %collective-permute-done.refs_1_, ...), custom_call_target="tpu_custom_call" | custom-call | flops 939524096 | bytes 6291456 | tf_op jit(solution)/shard_map/pallas_call | solution.py:293
  71.2 1.3 collective-permute-start.3
  72.5 9.9 %collective-permute-done.3.refs_0_ = bf16[256,512]{1,0:T(8,128)(2,1)S(1)} collective-permute-done((bf16[256,512]{1,0:T(8,128)(2,1)S(1)}, bf16[256,512]{1,0:T(8,128)(2,1)S(1)}, u32[]{:S(2)}, u32[]{:S(2)}) %collective-permute-start.3) | collective-permute-done | bytes 262176 | tf_op jit(solution)/shard_map/ppermute | solution.py:363
  82.4 1.3 collective-permute-start.7
  83.7 1.3 collective-permute-start.9
  85.0 7.3 %shard_map.116 = bf16[544,256]{1,0:T(8,128)(2,1)S(1)} custom-call(s32[2]{0:T(128)S(1)} %pad_add_fusion.ids, s32[8,12]{1,0:T(8,128)S(1)} %copy-done.6, bf16[256,512]{1,0:T(8,128)(2,1)S(1)} %collective-permute-done.3.refs_0_, bf16[1024,512]{1,0:T(8,128)(2,1)S(1)} %copy-done, bf16[1024,512]{1,0:T(8,128)(2,1)S(1)} %copy-done.1, ...), custom_call_target="tpu_custom_call" | custom-call | flops 1073741824 | bytes 4194304 | tf_op jit(solution)/shard_map/pallas_call | solution.py:342
  92.3 1.3 collective-permute-start.6
  93.6 1.7 %collective-permute-done.7.refs_0_ = bf16[256,512]{1,0:T(8,128)(2,1)S(1)} collective-permute-done((bf16[256,512]{1,0:T(8,128)(2,1)S(1)}, bf16[256,512]{1,0:T(8,128)(2,1)S(1)}, u32[]{:S(2)}, u32[]{:S(2)}) %collective-permute-start.7) | collective-permute-done | bytes 262176 | tf_op jit(solution)/shard_map/ppermute | solution.py:363
  95.4 7.3 %shard_map.117 = bf16[544,256]{1,0:T(8,128)(2,1)S(1)} custom-call(s32[2]{0:T(128)S(1)} %pad_add_fusion.ids, s32[8,12]{1,0:T(8,128)S(1)} %copy-done.6, bf16[256,512]{1,0:T(8,128)(2,1)S(1)} %collective-permute-done.7.refs_0_, bf16[1024,512]{1,0:T(8,128)(2,1)S(1)} %copy-done, bf16[1024,512]{1,0:T(8,128)(2,1)S(1)} %copy-done.1, ...), custom_call_target="tpu_custom_call" | custom-call | flops 1073741824 | bytes 4194304 | tf_op jit(solution)/shard_map/pallas_call | solution.py:342
  102.7 1.3 collective-permute-start.8
  104.0 7.3 %shard_map.118 = bf16[544,256]{1,0:T(8,128)(2,1)S(1)} custom-call(s32[2]{0:T(128)S(1)} %pad_add_fusion.ids, s32[8,12]{1,0:T(8,128)S(1)} %copy-done.6, bf16[256,512]{1,0:T(8,128)(2,1)S(1)} %collective-permute-done.9.refs_0_, bf16[1024,512]{1,0:T(8,128)(2,1)S(1)} %copy-done, bf16[1024,512]{1,0:T(8,128)(2,1)S(1)} %copy-done.1, ...), custom_call_target="tpu_custom_call" | custom-call | flops 1073741824 | bytes 4194304 | tf_op jit(solution)/shard_map/pallas_call | solution.py:342
  111.3 1.3 collective-permute-start.10
  112.6 4.0 %shard_map.115.refs_0_ = bf16[544,256]{1,0:T(8,128)(2,1)S(1)} custom-call(s32[2]{0:T(128)S(1)} %pad_add_fusion.ids, s32[8,12]{1,0:T(8,128)S(1)} %copy-done.6, s32[1,256]{1,0:T(1,128)S(1)} %bitcast.7, bf16[256,512]{1,0:T(8,128)(2,1)S(1)} %get-tuple-element.8.refs_1_.refs_0_, bf16[1024,512]{1,0:T(8,128)(2,1)S(1)} %copy-done, bf16[1024,512]{1,0:T(8,128)(2,1)S(1)} %copy-done.1), custom_call_target="tpu_custom_call" | custom-call | flops 536870912 | bytes 2097152 | tf_op jit(solution)/shard_map/pallas_call | solution.py:342
  116.6 0.0 copy-start.3
  116.6 0.0 copy-start.5
  116.6 4.1 %shard_map.119.refs_4_ = bf16[544,256]{1,0:T(8,128)(2,1)S(1)} custom-call(s32[2]{0:T(128)S(1)} %pad_add_fusion.ids, s32[8,12]{1,0:T(8,128)S(1)} %copy-done.6, bf16[256,512]{1,0:T(8,128)(2,1)S(1)} %get-tuple-element.8.refs_1_.refs_0_, bf16[1024,512]{1,0:T(8,128)(2,1)S(1)} %collective-permute-done.4.refs_3_.refs_1_, ...), custom_call_target="tpu_custom_call" | custom-call | flops 536870912 | bytes 2097152 | tf_op jit(solution)/shard_map/pallas_call | solution.py:342
  120.7 0.8 shard_map.120.refs_0_
  121.6 0.3 collective-permute-start.11
  121.9 0.9 collective-permute-start.12
  122.7 6.2 %collective-permute-done.11.refs_1_ = bf16[512,256]{1,0:T(8,128)(2,1)S(1)} collective-permute-done((bf16[512,256]{1,0:T(8,128)(2,1)S(1)}, bf16[512,256]{1,0:T(8,128)(2,1)S(1)}, u32[]{:S(2)}, u32[]{:S(2)}) %collective-permute-start.11) | collective-permute-done | bytes 262176 | tf_op jit(solution)/shard_map/ppermute | solution.py:228
  128.9 1.4 %collective-permute-start.13 = (bf16[512,256]{1,0:T(8,128)(2,1)S(1)}, bf16[512,256]{1,0:T(8,128)(2,1)S(1)}, u32[]{:S(2)}, u32[]{:S(2)}) collective-permute-start(bf16[512,256]{1,0:T(8,128)(2,1)S(1)} %collective-permute-done.11.refs_1_), channel_id=1, source_target_pairs={{0,1},{1,0},{2,3},{3,2},{4,5},{5,4},{6,7},{7,6},{8,9},{9,8},{10,11... | collective-permute-start | bytes 786440 | tf_op jit(solution)/shard_map/ppermute | solution.py:228
  130.3 1.2 collective-permute-done.13.refs_3_
  131.5 6.8 %shard_map.121 = (bf16[256,2048]{1,0:T(8,128)(2,1)}, bf16[64,2048]{1,0:T(8,128)(2,1)}) custom-call(s32[2]{0:T(128)S(1)} %pad_add_fusion.ids, bf16[512,256]{1,0:T(8,128)(2,1)S(1)} %shard_map.120.refs_0_, bf16[512,256]{1,0:T(8,128)(2,1)S(1)} %collective-permute-done.11.refs_1_, bf16[512,256]{1,0:T(8,128)(2,1)S(1)} %collective-permute-done.12.refs_2_, ...), custom_call_target="tpu_custom_call" | custom-call | flops 2147483648 | bytes 8388608 | tf_op jit(solution)/shard_map/pallas_call | solution.py:389
  (25 shorter events, 0.1 us)
Async XLA Ops:
  0.6 66.1 %copy-start.8 = (s32[1,256]{1,0:T(1,128)S(1)}, s32[1,256]{1,0:T(1,128)}, u32[]{:S(2)}) copy-start(s32[1,256]{1,0:T(1,128)} %refs_4_.1) | copy-start | bytes 3076
  0.6 66.0 %copy-start.10 = (f32[2048]{0:T(1024)S(1)}, f32[2048]{0:T(1024)}, u32[]{:S(2)}) copy-start(f32[2048]{0:T(1024)} %param.16) | copy-start | bytes 24580
  0.7 66.0 %copy-start.9 = (f32[2048]{0:T(1024)S(1)}, f32[2048]{0:T(1024)}, u32[]{:S(2)}) copy-start(f32[2048]{0:T(1024)} %param.15) | copy-start | bytes 24580
  0.7 1.2 copy-start.2
  2.0 0.7 copy-start.7
  2.6 64.0 %copy-start.11 = (s32[1,256]{1,0:T(1,128)S(1)}, s32[1,256]{1,0:T(1,128)}, u32[]{:S(2)}) copy-start(s32[1,256]{1,0:T(1,128)} %refs_5_.1) | copy-start | bytes 3076
  3.7 10.1 %collective-permute-start = (bf16[96,2048]{1,0:T(8,128)(2,1)S(1)}, bf16[96,2048]{1,0:T(8,128)(2,1)S(1)}, u32[]{:S(2)}, u32[]{:S(2)}) collective-permute-start(bf16[96,2048]{1,0:T(8,128)(2,1)S(1)} %shard_map.113.refs_0_), channel_id=1, source_target_pairs={{0,2},{1,3},{2,0},{3,1},{4,6},{5,7},{6,4},{7,5},{8,10},{9,11},{10,... | collective-permute-start | bytes 1179656 | tf_op jit(solution)/shard_map/ppermute | solution.py:228
  13.8 46.0 %collective-permute-start.14 = (bf16[512,2048]{1,0:T(8,128)(2,1)}, bf16[512,2048]{1,0:T(8,128)(2,1)}, u32[]{:S(2)}, u32[]{:S(2)}) collective-permute-start(bf16[512,2048]{1,0:T(8,128)(2,1)} %refs_4_.2), channel_id=1, source_target_pairs={{0,2},{1,3},{2,0},{3,1},{4,6},{5,7},{6,4},{7,5},{8,10},{9,11},{10,... | collective-permute-start | bytes 6291464 | tf_op jit(solution)/shard_map/ppermute | solution.py:228
  14.0 48.1 %collective-permute-start.1 = (bf16[96,2048]{1,0:T(8,128)(2,1)S(1)}, bf16[96,2048]{1,0:T(8,128)(2,1)S(1)}, u32[]{:S(2)}, u32[]{:S(2)}) collective-permute-start(bf16[96,2048]{1,0:T(8,128)(2,1)S(1)} %shard_map.113.refs_0_), channel_id=1, source_target_pairs={{0,1},{1,0},{2,3},{3,2},{4,5},{5,4},{6,7},{7,6},{8,9},{9,8},{10,11... | collective-permute-start | bytes 1179656 | tf_op jit(solution)/shard_map/ppermute | solution.py:228
  15.8 67.9 %collective-permute-start.4 = (bf16[1024,512]{1,0:T(8,128)(2,1)}, bf16[1024,512]{1,0:T(8,128)(2,1)S(1)}, u32[]{:S(2)}, u32[]{:S(2)}) collective-permute-start(bf16[1024,512]{1,0:T(8,128)(2,1)} %refs_1_.5), channel_id=1, source_target_pairs={{0,4},{4,0},{8,12},{12,8},{16,20},{20,16},{24,28},{28,24},{1,5},{5... | collective-permute-start | bytes 3145736 | tf_op jit(solution)/shard_map/ppermute | solution.py:274
  15.8 69.2 %collective-permute-start.5 = (bf16[1024,512]{1,0:T(8,128)(2,1)}, bf16[1024,512]{1,0:T(8,128)(2,1)S(1)}, u32[]{:S(2)}, u32[]{:S(2)}) collective-permute-start(bf16[1024,512]{1,0:T(8,128)(2,1)} %refs_2_.7), channel_id=1, source_target_pairs={{0,4},{4,0},{8,12},{12,8},{16,20},{20,16},{24,28},{28,24},{1,5},{5... | collective-permute-start | bytes 3145736 | tf_op jit(solution)/shard_map/ppermute | solution.py:275
  18.2 113.3 %collective-permute-start.15 = (bf16[512,2048]{1,0:T(8,128)(2,1)}, bf16[512,2048]{1,0:T(8,128)(2,1)S(1)}, u32[]{:S(2)}, u32[]{:S(2)}) collective-permute-start(bf16[512,2048]{1,0:T(8,128)(2,1)} %refs_4_.2), channel_id=1, source_target_pairs={{0,1},{1,0},{2,3},{3,2},{4,5},{5,4},{6,7},{7,6},{8,9},{9,8},{10,11... | collective-permute-start | bytes 6291464 | tf_op jit(solution)/shard_map/ppermute | solution.py:228
  59.7 71.8 %collective-permute-start.16 = (bf16[512,2048]{1,0:T(8,128)(2,1)}, bf16[512,2048]{1,0:T(8,128)(2,1)S(1)}, u32[]{:S(2)}, u32[]{:S(2)}) collective-permute-start(bf16[512,2048]{1,0:T(8,128)(2,1)} %collective-permute-done.14.refs_5_), channel_id=1, source_target_pairs={{0,1},{1,0},{2,3},{3,2},{4,5},{5,4},{6,7},{7,6},{8,9},{9,8},{10,11... | collective-permute-start | bytes 6291464 | tf_op jit(solution)/shard_map/ppermute | solution.py:228
  62.1 4.6 %collective-permute-start.2 = (bf16[96,2048]{1,0:T(8,128)(2,1)S(1)}, bf16[96,2048]{1,0:T(8,128)(2,1)S(1)}, u32[]{:S(2)}, u32[]{:S(2)}) collective-permute-start(bf16[96,2048]{1,0:T(8,128)(2,1)S(1)} %collective-permute-done.refs_1_), channel_id=1, source_target_pairs={{0,1},{1,0},{2,3},{3,2},{4,5},{5,4},{6,7},{7,6},{8,9},{9,8},{10,11... | collective-permute-start | bytes 1179656 | tf_op jit(solution)/shard_map/ppermute | solution.py:228
  62.8 22.3 %copy-start.6 = (s32[8,12]{1,0:T(8,128)S(1)}, s32[8,12]{1,0:T(8,128)}, u32[]{:S(2)}) copy-start(s32[8,12]{1,0:T(8,128)} %pattern.9) | copy-start | bytes 1156
  62.9 22.1 %copy-start = (bf16[1024,512]{1,0:T(8,128)(2,1)S(1)}, bf16[1024,512]{1,0:T(8,128)(2,1)}, u32[]{:S(2)}) copy-start(bf16[1024,512]{1,0:T(8,128)(2,1)} %refs_1_.5) | copy-start | bytes 3145732
  62.9 22.1 %copy-start.1 = (bf16[1024,512]{1,0:T(8,128)(2,1)S(1)}, bf16[1024,512]{1,0:T(8,128)(2,1)}, u32[]{:S(2)}) copy-start(bf16[1024,512]{1,0:T(8,128)(2,1)} %refs_2_.7) | copy-start | bytes 3145732
  66.7 1.6 %copy-start.4 = (bf16[2048,512]{1,0:T(8,128)(2,1)S(1)}, bf16[2048,512]{1,0:T(8,128)(2,1)}, u32[]{:S(2)}) copy-start(bf16[2048,512]{1,0:T(8,128)(2,1)} %refs_10_.1) | copy-start | bytes 6291460
  71.2 11.2 %collective-permute-start.3 = (bf16[256,512]{1,0:T(8,128)(2,1)S(1)}, bf16[256,512]{1,0:T(8,128)(2,1)S(1)}, u32[]{:S(2)}, u32[]{:S(2)}) collective-permute-start(bf16[256,512]{1,0:T(8,128)(2,1)S(1)} %get-tuple-element.8.refs_1_.refs_0_), channel_id=1, source_target_pairs={{24,0},{28,4},{25,1},{29,5},{26,2},{30,6},{27,3},{31,7}} | collective-permute-start | bytes 786440 | tf_op jit(solution)/shard_map/ppermute | solution.py:363
  82.4 13.0 %collective-permute-start.7 = (bf16[256,512]{1,0:T(8,128)(2,1)S(1)}, bf16[256,512]{1,0:T(8,128)(2,1)S(1)}, u32[]{:S(2)}, u32[]{:S(2)}) collective-permute-start(bf16[256,512]{1,0:T(8,128)(2,1)S(1)} %get-tuple-element.8.refs_1_.refs_0_), channel_id=1, source_target_pairs={{16,0},{20,4},{24,8},{28,12},{17,1},{21,5},{25,9},{29,13},{18,2},{... | collective-permute-start | bytes 786440 | tf_op jit(solution)/shard_map/ppermute | solution.py:363
  83.7 20.3 %collective-permute-start.9 = (bf16[256,512]{1,0:T(8,128)(2,1)S(1)}, bf16[256,512]{1,0:T(8,128)(2,1)S(1)}, u32[]{:S(2)}, u32[]{:S(2)}) collective-permute-start(bf16[256,512]{1,0:T(8,128)(2,1)S(1)} %get-tuple-element.8.refs_1_.refs_0_), channel_id=1, source_target_pairs={{8,0},{12,4},{16,8},{20,12},{24,16},{28,20},{9,1},{13,5},{17,9},{2... | collective-permute-start | bytes 786440 | tf_op jit(solution)/shard_map/ppermute | solution.py:363
  92.3 28.4 %collective-permute-start.6 = (bf16[544,256]{1,0:T(8,128)(2,1)S(1)}, bf16[544,256]{1,0:T(8,128)(2,1)S(1)}, u32[]{:S(2)}, u32[]{:S(2)}) collective-permute-start(bf16[544,256]{1,0:T(8,128)(2,1)S(1)} %shard_map.116), channel_id=1, source_target_pairs={{0,24},{4,28},{1,25},{5,29},{2,26},{6,30},{3,27},{7,31}} | collective-permute-start | bytes 835592 | tf_op jit(solution)/shard_map/ppermute | solution.py:370
  102.7 18.0 %collective-permute-start.8 = (bf16[544,256]{1,0:T(8,128)(2,1)S(1)}, bf16[544,256]{1,0:T(8,128)(2,1)S(1)}, u32[]{:S(2)}, u32[]{:S(2)}) collective-permute-start(bf16[544,256]{1,0:T(8,128)(2,1)S(1)} %shard_map.117), channel_id=1, source_target_pairs={{0,16},{4,20},{8,24},{12,28},{1,17},{5,21},{9,25},{13,29},{2,18},{... | collective-permute-start | bytes 835592 | tf_op jit(solution)/shard_map/ppermute | solution.py:370
  111.3 9.4 %collective-permute-start.10 = (bf16[544,256]{1,0:T(8,128)(2,1)S(1)}, bf16[544,256]{1,0:T(8,128)(2,1)S(1)}, u32[]{:S(2)}, u32[]{:S(2)}) collective-permute-start(bf16[544,256]{1,0:T(8,128)(2,1)S(1)} %shard_map.118), channel_id=1, source_target_pairs={{0,8},{4,12},{8,16},{12,20},{16,24},{20,28},{1,9},{5,13},{9,17},{1... | collective-permute-start | bytes 835592 | tf_op jit(solution)/shard_map/ppermute | solution.py:370
  116.6 14.9 %copy-start.3 = (bf16[256,2048]{1,0:T(8,128)(2,1)S(1)}, bf16[256,2048]{1,0:T(8,128)(2,1)}, u32[]{:S(2)}) copy-start(bf16[256,2048]{1,0:T(8,128)(2,1)} %refs_11_.1) | copy-start | bytes 3145732
  116.6 14.9 %copy-start.5 = (bf16[512,2048]{1,0:T(8,128)(2,1)S(1)}, bf16[512,2048]{1,0:T(8,128)(2,1)}, u32[]{:S(2)}) copy-start(bf16[512,2048]{1,0:T(8,128)(2,1)} %refs_4_.2) | copy-start | bytes 6291460
  121.6 7.3 %collective-permute-start.11 = (bf16[512,256]{1,0:T(8,128)(2,1)S(1)}, bf16[512,256]{1,0:T(8,128)(2,1)S(1)}, u32[]{:S(2)}, u32[]{:S(2)}) collective-permute-start(bf16[512,256]{1,0:T(8,128)(2,1)S(1)} %shard_map.120.refs_0_), channel_id=1, source_target_pairs={{0,2},{1,3},{2,0},{3,1},{4,6},{5,7},{6,4},{7,5},{8,10},{9,11},{10,... | collective-permute-start | bytes 786440 | tf_op jit(solution)/shard_map/ppermute | solution.py:228
  121.9 8.5 %collective-permute-start.12 = (bf16[512,256]{1,0:T(8,128)(2,1)S(1)}, bf16[512,256]{1,0:T(8,128)(2,1)S(1)}, u32[]{:S(2)}, u32[]{:S(2)}) collective-permute-start(bf16[512,256]{1,0:T(8,128)(2,1)S(1)} %shard_map.120.refs_0_), channel_id=1, source_target_pairs={{0,1},{1,0},{2,3},{3,2},{4,5},{5,4},{6,7},{7,6},{8,9},{9,8},{10,11... | collective-permute-start | bytes 786440 | tf_op jit(solution)/shard_map/ppermute | solution.py:228
  128.9 2.6 %collective-permute-start.13 = (bf16[512,256]{1,0:T(8,128)(2,1)S(1)}, bf16[512,256]{1,0:T(8,128)(2,1)S(1)}, u32[]{:S(2)}, u32[]{:S(2)}) collective-permute-start(bf16[512,256]{1,0:T(8,128)(2,1)S(1)} %collective-permute-done.11.refs_1_), channel_id=1, source_target_pairs={{0,1},{1,0},{2,3},{3,2},{4,5},{5,4},{6,7},{7,6},{8,9},{9,8},{10,11... | collective-permute-start | bytes 786440 | tf_op jit(solution)/shard_map/ppermute | solution.py:228
where the time goes:
time: 139 us; the launch traced here: 138 us
  waiting for transfers between devices  73.4 us (53%)
  Pallas kernels  41.5 us (30%)
  starting transfers between devices  17.3 us (12%)
  local copies, waits for them, and re-layouts  3.54 us (3%)
  other arithmetic  1.63 us (1%)
    ppermute x9, waiting for transfers between devices, gather_pack(): pieces = pieces + [lax.ppermute(held, 'pack', pairs) for held in pieces]  61.8 us
    pallas_call x5, Pallas kernels, attend(): run(functools.partial(attend_body, shift, use, n_ctx, chunk), grid=(route...  29.9 us
    ppermute x3, waiting for transfers between devices, local(): lax.ppermute(queries, 'ctx', [(c, c - 2 * shift) for c in range(2 * shift...  11.6 us
    ppermute x9, starting transfers between devices, gather_pack(): pieces = pieces + [lax.ppermute(held, 'pack', pairs) for held in pieces]  8.08 us
    pallas_call x1, Pallas kernels, local(): run(functools.partial(finish_body, n_pack), grid=(width // columns,), sca...  6.8 us
    ppermute x3, starting transfers between devices, local(): lax.ppermute(partial, 'ctx', [(c, c + 2 * shift) for c in range(n_ctx - 2...  3.92 us
    ppermute x3, starting transfers between devices, local(): lax.ppermute(queries, 'ctx', [(c, c - 2 * shift) for c in range(2 * shift...  3.86 us
    unnamed x24, local copies, waits for them, and re-layouts  3.54 us
  transfers between devices with their start and end apart: 17, of which 7 were waited for; matrix products, arithmetic and copies ran while one was open for 1% of the time, Pallas kernels for 24%

commit v1 on v0

v1 whole, which is shorter than its diff:
```python
import functools
import math

import jax
import jax.numpy as jnp
from jax import lax
from jax.experimental import pallas as pl
from jax.experimental.pallas import tpu as pltpu
from jax.sharding import PartitionSpec as P


HD = 128
EPS = 1e-06
NEG = -1e30
TAIL = 16
GROUPS = 2
SCALE = math.log2(math.e) / math.sqrt(HD)


def contract(left, right, left_dim, right_dim):
    return lax.dot_general(
        left, right, (((left_dim,), (right_dim,)), ((), ())), preferred_element_type=jnp.float32
    )


def run(body, *, grid, scalars, in_specs, out_specs, out_shape, scratch=(), cost=None, mib=16):
    kernel = call(body, grid, scalars, in_specs, out_specs, out_shape, scratch, cost, mib)

    return kernel


def call(body, grid, scalars, in_specs, out_specs, out_shape, scratch, cost, mib):
    return pl.pallas_call(
        body,
        grid_spec=pltpu.PrefetchScalarGridSpec(
            num_scalar_prefetch=scalars,
            grid=grid,
            in_specs=in_specs,
            out_specs=out_specs,
            scratch_shapes=list(scratch),
        ),
        out_shape=out_shape,
        cost_estimate=cost,
        compiler_params=pltpu.CompilerParams(vmem_limit_bytes=mib * 2**20),
    )


def cost_of(flops, moved, exps=0):
    return pl.CostEstimate(flops=int(flops), bytes_accessed=int(moved), transcendentals=int(exps))


def below(routes, bound):
    return jnp.sum(jnp.where(routes < bound, 1.0, 0.0), axis=1, keepdims=True).astype(jnp.int32)


def pick_body(ids, routes_ref, hidden_ref, out_ref):
    tok = hidden_ref.shape[0]
    cap = out_ref.shape[0]
    routed = routes_ref.shape[1]
    base = ids[1] * tok
    routes = routes_ref[...]
    token = lax.broadcasted_iota(jnp.int32, (tok, routed), 0) + base
    hit = jnp.where(routes == token, 1.0, 0.0).astype(jnp.bfloat16)
    entry = lax.broadcasted_iota(jnp.int32, (cap, routed), 1)
    slot = lax.broadcasted_iota(jnp.int32, (cap, routed), 0)
    choose = jnp.where(entry == slot + below(routes, base), 1.0, 0.0).astype(jnp.bfloat16)
    one_hot = contract(choose, hit, 1, 1).astype(jnp.bfloat16)
    out_ref[...] = contract(one_hot, hidden_ref[...], 1, 0).astype(out_ref.dtype)


def query_body(xors, tok, groups, ids, *refs):
    count = len(xors)
    pieces = refs[:count]
    routes_ref, order_ref, gain_ref, router_ref, cos_ref, sin_ref, wq_hbm = refs[count : count + 7]
    rows_ref, gate_ref = refs[count + 7 : count + 9]
    query_refs = refs[count + 9 : count + 9 + groups]
    wq_ref, sem = refs[count + 9 + groups :]
    load = pltpu.make_async_copy(wq_hbm, wq_ref, sem)
    load.start()
    cap = pieces[0].shape[0]
    routed = order_ref.shape[1]
    routes = routes_ref[...]
    order = order_ref[...]
    entry = lax.broadcasted_iota(jnp.int32, (cap, routed), 0)
    rows = None
    for xor, piece in zip(xors, pieces):
        owner = ids[1] ^ xor
        listed = entry + below(routes, owner * tok)
        stop = below(routes, (owner + 1) * tok)
        one_hot = jnp.where((order == listed) & (listed < stop), 1.0, 0.0).astype(jnp.bfloat16)
        term = contract(one_hot, piece[...], 0, 0)
        rows = term if rows is None else rows + term
    rows_ref[...] = rows.astype(rows_ref.dtype)
    logit = jnp.sum(rows * router_ref[...], axis=1, keepdims=True)
    gate_ref[...] = jnp.broadcast_to(1.0 / (1.0 + jnp.exp(-logit)), gate_ref.shape)
    mean_square = jnp.mean(rows * rows, axis=1, keepdims=True)
    normed = (rows * lax.rsqrt(mean_square + EPS) * gain_ref[...]).astype(jnp.bfloat16)
    load.wait()
    projected = contract(normed, wq_ref[...], 1, 0)
    cosine = cos_ref[...]
    sine = sin_ref[...]
    per = query_refs[0].shape[1] // HD
    for head in range(per * groups):
        part = projected[:, head * HD : (head + 1) * HD]
        turned = part * cosine + pltpu.roll(part, HD // 2, 1) * sine
        at = head % per * HD
        query_refs[head // per][:, at : at + HD] = turned.astype(jnp.bfloat16)


def split_body(group, keys_hbm, values_hbm, out_ref, sems):
    span, width = out_ref.shape[0] // 2, out_ref.shape[1]
    loads = [
        pltpu.make_async_copy(
            source.at[:, pl.ds(group * width, width)],
            out_ref.at[pl.ds(at * span, span), :],
            sems.at[at],
        )
        for at, source in enumerate((keys_hbm, values_hbm))
    ]
    for load in loads:
        load.start()
    for load in loads:
        load.wait()


def level_rows(part_ref, heads):
    tail = part_ref[heads * HD :, :].astype(jnp.float32)
    return [
        tail[head : head + 1] + tail[heads + head : heads + head + 1]
        + tail[2 * heads + head : 2 * heads + head + 1]
        for head in range(heads)
    ]


def attend_body(shift, use, prior, n_ctx, ids, pattern, *refs):
    masked_own = shift == 0 and "own" in use
    if masked_own:
        qpos_ref, refs = refs[0], refs[1:]
    if prior:
        prior_ref, refs = refs[0], refs[1:]
    q_ref, refs = refs[0], refs[1:]
    spans, refs = refs[: len(use)], refs[len(use) :]
    out_ref, m_ref, l_ref, acc_ref = refs
    span = spans[0].shape[0] // 2
    chunk = min(span, 1024)
    heads = q_ref.shape[1] // HD
    here = ids[0]
    source = here + 2 * shift
    row = jnp.minimum(source, n_ctx - 1)

    def attends(key_span):
        found = pattern[row, 0] == key_span
        for at in range(1, pattern.shape[1]):
            found = found | (pattern[row, at] == key_span)
        return found & (source < n_ctx) & (key_span < source)

    def block(kv_ref, masked, fresh):
        for at in range(0, span, chunk):
            for head in range(heads):
                cut = slice(head * HD, (head + 1) * HD)
                scores = contract(kv_ref[at : at + chunk, cut], q_ref[:, cut], 1, 1) * SCALE
                if masked:
                    kpos = lax.broadcasted_iota(jnp.int32, scores.shape, 0) + at
                    scores = jnp.where(kpos <= qpos_ref[...], scores, NEG)
                peak = jnp.max(scores, axis=0, keepdims=True)
                if not (fresh and at == 0):
                    former = m_ref[head : head + 1, :]
                    peak = jnp.maximum(former, peak)
                weights = jnp.exp2(scores - peak)
                total = jnp.sum(weights, axis=0, keepdims=True)
                value = contract(
                    kv_ref[span + at : span + at + chunk, cut], weights.astype(jnp.bfloat16), 0, 0
                )
                if not (fresh and at == 0):
                    fade = jnp.exp2(former - peak)
                    total = l_ref[head : head + 1, :] * fade + total
                    value = acc_ref[cut, :] * fade + value
                m_ref[head : head + 1, :] = peak
                l_ref[head : head + 1, :] = total
                acc_ref[cut, :] = value

    if masked_own:
        block(spans[0], True, True)
    else:
        if prior:
            for head, level in enumerate(level_rows(prior_ref, heads)):
                m_ref[head : head + 1, :] = level
                l_ref[head : head + 1, :] = jnp.where(level > 0.5 * NEG, 1.0, 0.0)
            acc_ref[...] = prior_ref[: heads * HD, :].astype(jnp.float32)
        else:
            m_ref[...] = jnp.full_like(m_ref, NEG)
            l_ref[...] = jnp.zeros_like(l_ref)
            acc_ref[...] = jnp.zeros_like(acc_ref)
        for kind, kv_ref in zip(use, spans):
            key_span = here if kind == "own" else here ^ 1
            pl.when(attends(key_span))(functools.partial(block, kv_ref, False, False))

    index = lax.broadcasted_iota(jnp.int32, (TAIL, out_ref.shape[1]), 0)
    tail = jnp.zeros(index.shape, jnp.float32)
    for head in range(heads):
        cut = slice(head * HD, (head + 1) * HD)
        total = l_ref[head : head + 1, :]
        some = total > 0.0
        safe = jnp.where(some, total, 1.0)
        out_ref[cut, :] = (acc_ref[cut, :] * (1.0 / safe)).astype(out_ref.dtype)
        rest = jnp.where(some, m_ref[head : head + 1, :] + jnp.log2(safe), NEG)
        for digit in range(3):
            value = rest.astype(jnp.bfloat16).astype(jnp.float32)
            tail = jnp.where(index == digit * heads + head, value, tail)
            rest = rest - value
    out_ref[heads * HD :, :] = tail.astype(out_ref.dtype)


def merge_body(shifts, ids, *refs):
    parts, out_ref = refs[:-1], refs[-1]
    heads = out_ref.shape[0] // HD
    levels = []
    for shift, part in zip(shifts, parts):
        rows = level_rows(part, heads)
        if shift:
            rows = [jnp.where(ids[0] >= 2 * shift, row, NEG) for row in rows]
        levels.append(rows)
    for head in range(heads):
        cut = slice(head * HD, (head + 1) * HD)
        mine = [rows[head] for rows in levels]
        peak = functools.reduce(jnp.maximum, mine)
        weights = [jnp.exp2(level - peak) for level in mine]
        inverse = 1.0 / functools.reduce(lambda a, b: a + b, weights)
        total = None
        for weight, part in zip(weights, parts):
            term = part[cut, :].astype(jnp.float32) * (weight * inverse)
            total = term if total is None else total + term
        out_ref[cut, :] = total.astype(out_ref.dtype)


def project(attended, weights, offset, columns):
    part = attended[0].shape[0]
    mixed = None
    for rows, weight in zip(attended, weights):
        term = contract(rows[...], weight[offset : offset + part, columns], 0, 0)
        mixed = term if mixed is None else mixed + term
    return mixed


def partial_body(count, offset, prior, *refs):
    attended, weights = refs[:count], refs[count : 2 * count]
    out_ref = refs[-1]
    width = out_ref.shape[1]
    step = min(512, width)
    for at in range(0, width, step):
        columns = slice(at, at + step)
        mixed = project(attended, weights, offset, columns)
        if prior:
            mixed = mixed + refs[2 * count][:, columns]
        out_ref[:, columns] = mixed


def finish_body(count, offset, ids, *refs):
    attended, weights = refs[:count], refs[count : 2 * count]
    sum_ref, rows_ref, gate_ref, picked_ref, hidden_ref = refs[2 * count : 2 * count + 5]
    hidden_out, packed_out, new_ref = refs[2 * count + 5 :]
    tok = hidden_ref.shape[0]
    routed = rows_ref.shape[0]
    own = packed_out.shape[0]
    step = hidden_out.shape[1]
    columns = pl.ds(pl.multiple_of(pl.program_id(0) * step, step), step)
    token = lax.broadcasted_iota(jnp.int32, (tok, routed), 0) + ids[1] * tok
    place = jnp.where(picked_ref[...] == token, 1.0, 0.0)
    filled = jnp.sum(place, axis=1, keepdims=True) > 0.0
    mixed = project(attended, weights, offset, columns) + sum_ref[:, columns]
    new = rows_ref[:, columns].astype(jnp.float32) + gate_ref[:, 0:1] * mixed
    new_ref[...] = new.astype(new_ref.dtype)
    packed_out[...] = new_ref[pl.ds(pl.multiple_of(ids[1] * own, own), own), :]
    moved = contract(place.astype(jnp.bfloat16), new_ref[...], 1, 0)
    hidden_out[...] = jnp.where(
        filled, moved, hidden_ref[:, columns].astype(jnp.float32)
    ).astype(hidden_out.dtype)


def gather_pack(piece, n_pack):
    pieces, xors = [piece], [0]
    bit = n_pack // 2
    while bit:
        pairs = [(p, p ^ bit) for p in range(n_pack)]
        pieces = pieces + [lax.ppermute(held, "pack", pairs) for held in pieces]
        xors = xors + [x ^ bit for x in xors]
        bit //= 2
    return pieces, xors


def local(
    hidden,
    first_keys,
    first_values,
    w_query,
    w_out,
    norm_gain,
    router_weight,
    route_list,
    pack_order,
    pattern,
):
    n_ctx = lax.axis_size("ctx")
    n_pack = lax.axis_size("pack")
    ctx = lax.axis_index("ctx")
    pack = lax.axis_index("pack")
    tok, width = hidden.shape
    span, part = first_keys.shape
    routed = route_list.shape[1]
    own = routed // n_pack
    cap = 3 * tok // 8
    group_width = part // GROUPS
    tall = group_width + TAIL
    ids = jnp.stack([ctx, pack]).astype(jnp.int32)
    whole = lambda shape: pl.BlockSpec(shape, lambda *_: (0,) * len(shape))
    in_hbm = pl.BlockSpec(memory_space=pltpu.HBM)
    bf16, f32 = jnp.bfloat16, jnp.float32
    shape_of = jax.ShapeDtypeStruct

    held = []
    for group in range(GROUPS):
        held.append(
            run(
                functools.partial(split_body, group),
                grid=(1,),
                scalars=0,
                in_specs=[in_hbm, in_hbm],
                out_specs=whole((2 * span, group_width)),
                out_shape=shape_of((2 * span, group_width), bf16),
                scratch=[pltpu.SemaphoreType.DMA((2,))],
                cost=cost_of(0, 8 * span * group_width),
            )(first_keys, first_values)
        )
    swap = [(c, c ^ 1) for c in range(n_ctx)]
    across = [lax.ppermute(kv, "ctx", swap) for kv in held]

    outgoing = run(
        pick_body,
        grid=(1,),
        scalars=1,
        in_specs=[whole((1, routed)), whole((tok, width))],
        out_specs=whole((cap, width)),
        out_shape=shape_of((cap, width), bf16),
        cost=cost_of(2 * cap * tok * width, 2 * tok * width * 2),
    )(ids, route_list, hidden)
    pieces, xors = gather_pack(outgoing, n_pack)

    picked = jnp.sum(
        jnp.where(
            pack_order[0][:, None] == jnp.arange(routed, dtype=jnp.int32)[None, :],
            route_list[0][None, :],
            0,
        ),
        axis=1,
    )
    position = picked + ctx * span
    half = HD // 2
    frequency = 10000.0 ** (-jnp.arange(half, dtype=f32) * 2.0 / HD)
    angle = position.astype(f32)[:, None] * frequency[None, :]
    cosine, sine = jnp.cos(angle), jnp.sin(angle)
    cosine = jnp.concatenate([cosine, cosine], axis=1)
    sine = jnp.concatenate([-sine, sine], axis=1)

    rows, gate, *queries = run(
        functools.partial(query_body, xors, tok, GROUPS),
        grid=(1,),
        scalars=1,
        in_specs=[whole((cap, width))] * n_pack
        + [
            whole((1, routed)),
            whole((1, routed)),
            whole((1, width)),
            whole((1, width)),
            whole((routed, HD)),
            whole((routed, HD)),
            in_hbm,
        ],
        out_specs=[whole((routed, width)), whole((routed, HD))]
        + [whole((routed, group_width))] * GROUPS,
        out_shape=[shape_of((routed, width), bf16), shape_of((routed, HD), f32)]
        + [shape_of((routed, group_width), bf16)] * GROUPS,
        scratch=[pltpu.VMEM((width, part), bf16), pltpu.SemaphoreType.DMA],
        cost=cost_of(2 * routed * width * (part + n_pack * cap), 6 * width * part),
        mib=32,
    )(
        ids,
        *pieces,
        route_list,
        pack_order,
        norm_gain.reshape(1, width),
        router_weight.reshape(1, width),
        cosine,
        sine,
        w_query,
    )

    w_in, _ = lax.optimization_barrier((w_out, pieces[1]))
    w_pieces, _ = gather_pack(w_in, n_pack)

    def attend(group, shift, query, use, prior=None):
        masked = shift == 0 and "own" in use
        given = [picked.reshape(1, routed)] if masked else []
        specs = [whole((1, routed))] if masked else []
        if prior is not None:
            given.append(prior)
            specs.append(whole((tall, routed)))
        arrays = [held[group] if kind == "own" else across[group] for kind in use]
        return run(
            functools.partial(attend_body, shift, use, prior is not None, n_ctx),
            grid=(1,),
            scalars=2,
            in_specs=specs
            + [whole((routed, group_width))]
            + [whole((2 * span, group_width))] * len(arrays),
            out_specs=whole((tall, routed)),
            out_shape=shape_of((tall, routed), bf16),
            scratch=[
                pltpu.VMEM((8, routed), f32),
                pltpu.VMEM((8, routed), f32),
                pltpu.VMEM((group_width, routed), f32),
            ],
            cost=cost_of(4 * len(use) * routed * span * group_width, 4 * span * group_width),
        )(ids, pattern, *given, query, *arrays)

    shifts = list(range(n_ctx // 2 - 1, 0, -1))
    attended = []
    for group in range(GROUPS):
        query = queries[group]
        first = attend(group, 0, query, ("own",))
        returned = []
        for shift in shifts:
            arrived = lax.ppermute(
                query, "ctx", [(c, c - 2 * shift) for c in range(2 * shift, n_ctx)]
            )
            if group < GROUPS - 1:
                partial = attend(group, shift, arrived, ("own", "other"))
            else:
                early = attend(group, shift, arrived, ("own",))
                partial = attend(group, shift, arrived, ("other",), early)
            returned.append(
                lax.ppermute(partial, "ctx", [(c, c + 2 * shift) for c in range(n_ctx - 2 * shift)])
            )
        second = attend(group, 0, query, ("other",), first)
        attended.append(
            run(
                functools.partial(merge_body, [0, *shifts]),
                grid=(1,),
                scalars=1,
                in_specs=[whole((tall, routed))] * (1 + len(shifts)),
                out_specs=whole((group_width, routed)),
                out_shape=shape_of((group_width, routed), bf16),
                cost=cost_of(8 * routed * group_width, 2 * tall * routed * (1 + len(shifts))),
            )(ids, second, *returned)
        )

    mixed = [gather_pack(value, n_pack)[0] for value in attended]

    def project_part(at, chosen, offset, prior):
        count = len(chosen)
        given = [] if prior is None else [prior]
        return run(
            functools.partial(partial_body, count, offset, prior is not None),
            grid=(1,),
            scalars=0,
            in_specs=[whole((group_width, routed))] * count
            + [whole((part, width))] * count
            + [whole((routed, width))] * len(given),
            out_specs=whole((routed, width)),
            out_shape=shape_of((routed, width), f32),
            cost=cost_of(2 * count * routed * group_width * width, 4 * routed * width),
        )(*[mixed[at][i] for i in chosen], *[w_pieces[i] for i in chosen], *given)

    total = None
    for group in range(GROUPS - 1):
        total = project_part(group, list(range(n_pack)), group * group_width, total)
    last = GROUPS - 1
    near = [i for i, x in enumerate(xors) if x < 2]
    distant = [i for i, x in enumerate(xors) if x >= 2]
    total = project_part(last, near, last * group_width, total)

    columns = width // 4
    hidden_out, packed = run(
        functools.partial(finish_body, len(distant), last * group_width),
        grid=(width // columns,),
        scalars=1,
        in_specs=[whole((group_width, routed))] * len(distant)
        + [whole((part, width))] * len(distant)
        + [
            whole((routed, width)),
            whole((routed, width)),
            whole((routed, HD)),
            whole((1, routed)),
            whole((tok, width)),
        ],
        out_specs=[
            pl.BlockSpec((tok, columns), lambda j, *_: (0, j)),
            pl.BlockSpec((own, columns), lambda j, *_: (0, j)),
        ],
        out_shape=[shape_of((tok, width), hidden.dtype), shape_of((own, width), hidden.dtype)],
        scratch=[pltpu.VMEM((routed, columns), bf16)],
        cost=cost_of(routed * width * width, 2 * width * width),
    )(
        ids,
        *[mixed[last][i] for i in distant],
        *[w_pieces[i] for i in distant],
        total,
        rows,
        gate,
        picked.reshape(1, routed),
        hidden,
    )
    return (hidden_out, packed)


def solution(mesh):
    return jax.shard_map(
        local,
        mesh=mesh,
        in_specs=(
            P(("ctx", "pack"), None),
            P("ctx", "pack"),
            P("ctx", "pack"),
            P(None, "pack"),
            P("pack", None),
            P(),
            P(),
            P("ctx", None),
            P("ctx", None),
            P(),
        ),
        out_specs=(P(("ctx", "pack"), None), P(("ctx", "pack"), None)),
        check_vma=False,
    )
```

time: 139 us -> 173 us (1.24)
  the two profiles are of different devices: /device:TPU:7 before, /device:TPU:5 now
where the time goes in v1:
time: 173 us; the launch traced here: 172 us
  waiting for transfers between devices  76.9 us (44%)
  Pallas kernels  52.1 us (30%)
  starting transfers between devices  36.6 us (21%)
  local copies, waits for them, and re-layouts  4.46 us (3%)
    ppermute x12, waiting for transfers between devices, gather_pack(): pieces = pieces + [lax.ppermute(held, 'pack', pairs) for held in pieces]  51.7 us
    pallas_call x13, Pallas kernels, attend(): run(functools.partial(attend_body, shift, use, prior is not None, n_ctx),...  31.7 us
    ppermute x6, waiting for transfers between devices, local(): lax.ppermute(query, 'ctx', [(c, c - 2 * shift) for c in range(2 * shift,...  25.1 us
    ppermute x12, starting transfers between devices, gather_pack(): pieces = pieces + [lax.ppermute(held, 'pack', pairs) for held in pieces]  19.3 us
    ppermute x6, starting transfers between devices, local(): lax.ppermute(partial, 'ctx', [(c, c + 2 * shift) for c in range(n_ctx - 2...  9 us
    pallas_call x2, Pallas kernels, project_part(): run(functools.partial(partial_body, count, offset, prior is not None), gr...  7.79 us
    ppermute x6, starting transfers between devices, local(): lax.ppermute(query, 'ctx', [(c, c - 2 * shift) for c in range(2 * shift,...  7.71 us
    pallas_call x1, Pallas kernels, local(): run(functools.partial(finish_body, len(distant), last * group_width), gri...  5.89 us
  transfers between devices with their start and end apart: 26, of which 8 were waited for; matrix products, arithmetic and copies ran while one was open for 1% of the time, Pallas kernels for 26%

profile of v1, /device:TPU:5, one launch (start us, length us, event | category | flops | bytes accessed | tf_op | source)
XLA Modules:
  0.0 172.1 jit_solution(2320234401841247215)
XLA Ops:
  0.7 1.3 copy-done.3
  2.0 0.7 copy-done.9
  2.7 1.0 shard_map.113.refs_0_
  3.7 1.3 collective-permute-start
  5.0 8.8 %collective-permute-done.refs_1_ = bf16[96,2048]{1,0:T(8,128)(2,1)S(1)} collective-permute-done((bf16[96,2048]{1,0:T(8,128)(2,1)S(1)}, bf16[96,2048]{1,0:T(8,128)(2,1)S(1)}, u32[]{:S(2)}, u32[]{:S(2)}) %collective-permute-start) | collective-permute-done | bytes 393248 | tf_op jit(solution)/shard_map/ppermute | solution.py:285
  13.8 1.2 collective-permute-start.12
  15.0 1.8 %collective-permute-start.1 = (bf16[96,2048]{1,0:T(8,128)(2,1)S(1)}, bf16[96,2048]{1,0:T(8,128)(2,1)}, u32[]{:S(2)}, u32[]{:S(2)}) collective-permute-start(bf16[96,2048]{1,0:T(8,128)(2,1)S(1)} %shard_map.113.refs_0_), channel_id=1, source_target_pairs={{0,1},{1,0},{2,3},{3,2},{4,5},{5,4},{6,7},{7,6},{8,9},{9,8},{10,11... | collective-permute-start | bytes 1179656 | tf_op jit(solution)/shard_map/ppermute | solution.py:285
  16.8 1.2 copy-done.1
  18.7 41.0 %collective-permute-done.12.refs_5_.refs_2_ = bf16[512,2048]{1,0:T(8,128)(2,1)} collective-permute-done((bf16[512,2048]{1,0:T(8,128)(2,1)}, bf16[512,2048]{1,0:T(8,128)(2,1)}, u32[]{:S(2)}, u32[]{:S(2)}) %collective-permute-start.12) | collective-permute-done | bytes 2097184 | tf_op jit(solution)/shard_map/ppermute | solution.py:285
  59.8 2.4 %collective-permute-start.13 = (bf16[512,2048]{1,0:T(8,128)(2,1)}, bf16[512,2048]{1,0:T(8,128)(2,1)}, u32[]{:S(2)}, u32[]{:S(2)}) collective-permute-start(bf16[512,2048]{1,0:T(8,128)(2,1)} %collective-permute-done.12.refs_5_.refs_2_), channel_id=1, source_target_pairs={{0,1},{1,0},{2,3},{3,2},{4,5},{5,4},{6,7},{7,6},{8,9},{9,8},{10,11... | collective-permute-start | bytes 6291464 | tf_op jit(solution)/shard_map/ppermute | solution.py:285
  62.5 1.2 copy-done.2
  64.8 1.9 %collective-permute-done.2.refs_3_ = bf16[96,2048]{1,0:T(8,128)(2,1)S(1)} collective-permute-done((bf16[96,2048]{1,0:T(8,128)(2,1)}, bf16[96,2048]{1,0:T(8,128)(2,1)S(1)}, u32[]{:S(2)}, u32[]{:S(2)}) %collective-permute-start.2) | collective-permute-done | bytes 393248 | tf_op jit(solution)/shard_map/ppermute | solution.py:285
  66.7 4.2 %shard_map.114 = (bf16[256,2048]{1,0:T(8,128)(2,1)S(1)}, f32[256,128]{1,0:T(8,128)S(1)}, bf16[256,256]{1,0:T(8,128)(2,1)S(1)}, bf16[256,256]{1,0:T(8,128)(2,1)S(1)}) custom-call(s32[2]{0:T(128)S(1)} %pad_add_fusion.ids, bf16[96,2048]{1,0:T(8,128)(2,1)S(1)} %shard_map.113.refs_0_, bf16[96,2048]{1,0:T(8,128)(2,1)S(1)} %copy-done.8, ...), custom_call_target="tpu_custom_call" | custom-call | flops 939524096 | bytes 6291456 | tf_op jit(solution)/shard_map/pallas_call | solution.py:364
  71.0 1.3 collective-permute-start.8
  72.3 5.3 %collective-permute-done.8.refs_0_.refs_1_ = bf16[256,256]{1,0:T(8,128)(2,1)S(1)} collective-permute-done((bf16[256,256]{1,0:T(8,128)(2,1)S(1)}, bf16[256,256]{1,0:T(8,128)(2,1)S(1)}, u32[]{:S(2)}, u32[]{:S(2)}) %collective-permute-start.8) | collective-permute-done | bytes 131104 | tf_op jit(solution)/shard_map/ppermute | solution.py:432
  77.5 1.3 collective-permute-start.6
  78.8 8.7 %collective-permute-done.6.refs_0_.refs_1_ = bf16[256,256]{1,0:T(8,128)(2,1)S(1)} collective-permute-done((bf16[256,256]{1,0:T(8,128)(2,1)S(1)}, bf16[256,256]{1,0:T(8,128)(2,1)S(1)}, u32[]{:S(2)}, u32[]{:S(2)}) %collective-permute-start.6) | collective-permute-done | bytes 131104 | tf_op jit(solution)/shard_map/ppermute | solution.py:432
  87.5 1.3 collective-permute-start.21
  88.8 4.4 %collective-permute-done.21.refs_0_ = bf16[256,256]{1,0:T(8,128)(2,1)S(1)} collective-permute-done((bf16[256,256]{1,0:T(8,128)(2,1)S(1)}, bf16[256,256]{1,0:T(8,128)(2,1)S(1)}, u32[]{:S(2)}, u32[]{:S(2)}) %collective-permute-start.21) | collective-permute-done | bytes 131104 | tf_op jit(solution)/shard_map/ppermute | solution.py:432
  93.2 1.3 collective-permute-start.17
  94.5 6.2 %collective-permute-done.17.refs_0_ = bf16[256,256]{1,0:T(8,128)(2,1)S(1)} collective-permute-done((bf16[256,256]{1,0:T(8,128)(2,1)S(1)}, bf16[256,256]{1,0:T(8,128)(2,1)S(1)}, u32[]{:S(2)}, u32[]{:S(2)}) %collective-permute-start.17) | collective-permute-done | bytes 131104 | tf_op jit(solution)/shard_map/ppermute | solution.py:432
  100.7 1.3 collective-permute-start.19
  102.0 1.3 collective-permute-start.4
  103.3 3.5 %shard_map.128 = bf16[272,256]{1,0:T(8,128)(2,1)S(1)} custom-call(s32[2]{0:T(128)S(1)} %pad_add_fusion.ids, s32[8,12]{1,0:T(8,128)S(1)} %copy-done.6, bf16[256,256]{1,0:T(8,128)(2,1)S(1)} %collective-permute-done.17.refs_0_, bf16[2048,256]{1,0:T(8,128)(2,1)S(1)} %shard_map.125.refs_2_.refs_1_, bf16[2048,256]{1,0:T(8,128)(2,1)S(1)} %collective-permute-done.16.refs_2_), custom_call_target="tpu_custom_call" | custom-call | flops 536870912 | bytes 1048576 | tf_op jit(solution)/shard_map/pallas_call | solution.py:408
  107.3 2.5 %collective-permute-start.18 = (bf16[272,256]{1,0:T(8,128)(2,1)S(1)}, bf16[272,256]{1,0:T(8,128)(2,1)S(1)}, u32[]{:S(2)}, u32[]{:S(2)}) collective-permute-start(bf16[272,256]{1,0:T(8,128)(2,1)S(1)} %shard_map.128), channel_id=1, source_target_pairs={{0,24},{4,28},{1,25},{5,29},{2,26},{6,30},{3,27},{7,31}} | collective-permute-start | bytes 417800 | tf_op jit(solution)/shard_map/ppermute | solution.py:441
  109.9 3.5 %shard_map.130 = bf16[272,256]{1,0:T(8,128)(2,1)S(1)} custom-call(s32[2]{0:T(128)S(1)} %pad_add_fusion.ids, s32[8,12]{1,0:T(8,128)S(1)} %copy-done.6, bf16[256,256]{1,0:T(8,128)(2,1)S(1)} %collective-permute-done.21.refs_0_, bf16[2048,256]{1,0:T(8,128)(2,1)S(1)} %shard_map.125.refs_2_.refs_1_, bf16[2048,256]{1,0:T(8,128)(2,1)S(1)} %collective-permute-done.16.refs_2_), custom_call_target="tpu_custom_call" | custom-call | flops 536870912 | bytes 1048576 | tf_op jit(solution)/shard_map/pallas_call | solution.py:408
  113.3 3.5 %shard_map.129 = bf16[272,256]{1,0:T(8,128)(2,1)S(1)} custom-call(s32[2]{0:T(128)S(1)} %pad_add_fusion.ids, s32[8,12]{1,0:T(8,128)S(1)} %copy-done.6, bf16[256,256]{1,0:T(8,128)(2,1)S(1)} %collective-permute-done.19.refs_0_, bf16[2048,256]{1,0:T(8,128)(2,1)S(1)} %shard_map.125.refs_2_.refs_1_, bf16[2048,256]{1,0:T(8,128)(2,1)S(1)} %collective-permute-done.16.refs_2_), custom_call_target="tpu_custom_call" | custom-call | flops 536870912 | bytes 1048576 | tf_op jit(solution)/shard_map/pallas_call | solution.py:408
  116.8 1.3 collective-permute-start.20
  118.1 1.3 collective-permute-start.22
  119.4 2.2 %shard_map.118.refs_0_ = bf16[272,256]{1,0:T(8,128)(2,1)S(1)} custom-call(s32[2]{0:T(128)S(1)} %pad_add_fusion.ids, s32[8,12]{1,0:T(8,128)S(1)} %copy-done.6, bf16[256,256]{1,0:T(8,128)(2,1)S(1)} %collective-permute-done.4.refs_0_.refs_1_, bf16[2048,256]{1,0:T(8,128)(2,1)S(1)} %shard_map.115.refs_2_.refs_1_), custom_call_target="tpu_custom_call" | custom-call | flops 268435456 | bytes 1048576 | tf_op jit(solution)/shard_map/pallas_call | solution.py:408
  121.7 2.1 %shard_map.119 = bf16[272,256]{1,0:T(8,128)(2,1)S(1)} custom-call(s32[2]{0:T(128)S(1)} %pad_add_fusion.ids, s32[8,12]{1,0:T(8,128)S(1)} %copy-done.6, bf16[272,256]{1,0:T(8,128)(2,1)S(1)} %shard_map.118.refs_0_, bf16[256,256]{1,0:T(8,128)(2,1)S(1)} %collective-permute-done.4.refs_0_.refs_1_, bf16[2048,256]{1,0:T(8,128)(2,1)S(1)} %collective-permute-done.3.refs_2_), custom_call_target="tpu_custom_call" | custom-call | flops 268435456 | bytes 1048576 | tf_op jit(solution)/shard_map/pallas_call | solution.py:408
  123.8 1.3 collective-permute-start.5
  125.1 2.1 %shard_map.122.refs_0_ = bf16[272,256]{1,0:T(8,128)(2,1)S(1)} custom-call(s32[2]{0:T(128)S(1)} %pad_add_fusion.ids, s32[8,12]{1,0:T(8,128)S(1)} %copy-done.6, bf16[256,256]{1,0:T(8,128)(2,1)S(1)} %collective-permute-done.8.refs_0_.refs_1_, bf16[2048,256]{1,0:T(8,128)(2,1)S(1)} %shard_map.115.refs_2_.refs_1_), custom_call_target="tpu_custom_call" | custom-call | flops 268435456 | bytes 1048576 | tf_op jit(solution)/shard_map/pallas_call | solution.py:408
  127.1 2.1 %shard_map.120.refs_0_ = bf16[272,256]{1,0:T(8,128)(2,1)S(1)} custom-call(s32[2]{0:T(128)S(1)} %pad_add_fusion.ids, s32[8,12]{1,0:T(8,128)S(1)} %copy-done.6, bf16[256,256]{1,0:T(8,128)(2,1)S(1)} %collective-permute-done.6.refs_0_.refs_1_, bf16[2048,256]{1,0:T(8,128)(2,1)S(1)} %shard_map.115.refs_2_.refs_1_), custom_call_target="tpu_custom_call" | custom-call | flops 268435456 | bytes 1048576 | tf_op jit(solution)/shard_map/pallas_call | solution.py:408
  129.2 2.1 %shard_map.123 = bf16[272,256]{1,0:T(8,128)(2,1)S(1)} custom-call(s32[2]{0:T(128)S(1)} %pad_add_fusion.ids, s32[8,12]{1,0:T(8,128)S(1)} %copy-done.6, bf16[272,256]{1,0:T(8,128)(2,1)S(1)} %shard_map.122.refs_0_, bf16[256,256]{1,0:T(8,128)(2,1)S(1)} %collective-permute-done.8.refs_0_.refs_1_, bf16[2048,256]{1,0:T(8,128)(2,1)S(1)} %collective-permute-done.3.refs_2_), custom_call_target="tpu_custom_call" | custom-call | flops 268435456 | bytes 1048576 | tf_op jit(solution)/shard_map/pallas_call | solution.py:408
  131.3 2.1 %shard_map.121 = bf16[272,256]{1,0:T(8,128)(2,1)S(1)} custom-call(s32[2]{0:T(128)S(1)} %pad_add_fusion.ids, s32[8,12]{1,0:T(8,128)S(1)} %copy-done.6, bf16[272,256]{1,0:T(8,128)(2,1)S(1)} %shard_map.120.refs_0_, bf16[256,256]{1,0:T(8,128)(2,1)S(1)} %collective-permute-done.6.refs_0_.refs_1_, bf16[2048,256]{1,0:T(8,128)(2,1)S(1)} %collective-permute-done.3.refs_2_), custom_call_target="tpu_custom_call" | custom-call | flops 268435456 | bytes 1048576 | tf_op jit(solution)/shard_map/pallas_call | solution.py:408
  133.3 1.3 collective-permute-start.7
  134.7 1.3 collective-permute-start.9
  136.0 2.2 %shard_map.126.refs_0_ = bf16[272,256]{1,0:T(8,128)(2,1)S(1)} custom-call(s32[2]{0:T(128)S(1)} %pad_add_fusion.ids, s32[8,12]{1,0:T(8,128)S(1)} %copy-done.6, s32[1,256]{1,0:T(1,128)S(1)} %bitcast.7, bf16[256,256]{1,0:T(8,128)(2,1)S(1)} %get-tuple-element.9.refs_1_, bf16[2048,256]{1,0:T(8,128)(2,1)S(1)} %shard_map.125.refs_2_.refs_1_), custom_call_target="tpu_custom_call" | custom-call | flops 268435456 | bytes 1048576 | tf_op jit(solution)/shard_map/pallas_call | solution.py:408
  138.1 2.1 %shard_map.127.refs_0_ = bf16[272,256]{1,0:T(8,128)(2,1)S(1)} custom-call(s32[2]{0:T(128)S(1)} %pad_add_fusion.ids, s32[8,12]{1,0:T(8,128)S(1)} %copy-done.6, bf16[272,256]{1,0:T(8,128)(2,1)S(1)} %shard_map.126.refs_0_, bf16[256,256]{1,0:T(8,128)(2,1)S(1)} %get-tuple-element.9.refs_1_, bf16[2048,256]{1,0:T(8,128)(2,1)S(1)} %collective-permute-done.16.refs_2_), custom_call_target="tpu_custom_call" | custom-call | flops 268435456 | bytes 1048576 | tf_op jit(solution)/shard_map/pallas_call | solution.py:408
  140.9 1.3 collective-permute-start.23
  142.2 2.2 %shard_map.116.refs_0_ = bf16[272,256]{1,0:T(8,128)(2,1)S(1)} custom-call(s32[2]{0:T(128)S(1)} %pad_add_fusion.ids, s32[8,12]{1,0:T(8,128)S(1)} %copy-done.6, s32[1,256]{1,0:T(1,128)S(1)} %bitcast.8, bf16[256,256]{1,0:T(8,128)(2,1)S(1)} %get-tuple-element.7.refs_1_, bf16[2048,256]{1,0:T(8,128)(2,1)S(1)} %shard_map.115.refs_2_.refs_1_), custom_call_target="tpu_custom_call" | custom-call | flops 268435456 | bytes 1048576 | tf_op jit(solution)/shard_map/pallas_call | solution.py:408
  144.3 2.3 %shard_map.117.refs_0_ = bf16[272,256]{1,0:T(8,128)(2,1)S(1)} custom-call(s32[2]{0:T(128)S(1)} %pad_add_fusion.ids, s32[8,12]{1,0:T(8,128)S(1)} %copy-done.6, bf16[272,256]{1,0:T(8,128)(2,1)S(1)} %shard_map.116.refs_0_, bf16[256,256]{1,0:T(8,128)(2,1)S(1)} %get-tuple-element.7.refs_1_, bf16[2048,256]{1,0:T(8,128)(2,1)S(1)} %collective-permute-done.3.refs_2_), custom_call_target="tpu_custom_call" | custom-call | flops 268435456 | bytes 1048576 | tf_op jit(solution)/shard_map/pallas_call | solution.py:408
  147.7 6.2 %collective-permute-start.24 = (bf16[256,256]{1,0:T(8,128)(2,1)S(1)}, bf16[256,256]{1,0:T(8,128)(2,1)S(1)}, u32[]{:S(2)}, u32[]{:S(2)}) collective-permute-start(bf16[256,256]{1,0:T(8,128)(2,1)S(1)} %shard_map.131.refs_0_), channel_id=1, source_target_pairs={{0,1},{1,0},{2,3},{3,2},{4,5},{5,4},{6,7},{7,6},{8,9},{9,8},{10,11... | collective-permute-start | bytes 393224 | tf_op jit(solution)/shard_map/ppermute | solution.py:285
  153.9 4.4 %collective-permute-start.14 = (bf16[256,256]{1,0:T(8,128)(2,1)S(1)}, bf16[256,256]{1,0:T(8,128)(2,1)S(1)}, u32[]{:S(2)}, u32[]{:S(2)}) collective-permute-start(bf16[256,256]{1,0:T(8,128)(2,1)S(1)} %shard_map.124.refs_0_), channel_id=1, source_target_pairs={{0,1},{1,0},{2,3},{3,2},{4,5},{5,4},{6,7},{7,6},{8,9},{9,8},{10,11... | collective-permute-start | bytes 393224 | tf_op jit(solution)/shard_map/ppermute | solution.py:285
  158.4 4.7 %shard_map.132.refs_4_ = f32[256,2048]{1,0:T(8,128)S(1)} custom-call(bf16[256,256]{1,0:T(8,128)(2,1)S(1)} %shard_map.131.refs_0_, bf16[256,256]{1,0:T(8,128)(2,1)S(1)} %collective-permute-done.23.refs_1_, bf16[256,256]{1,0:T(8,128)(2,1)S(1)} %collective-permute-done.24.refs_2_, bf16[256,256]{1,0:T(8,128)(2,1)S(1)} %collective-permute-done.25.refs_3_, ...), custom_call_target="tpu_custom_call" | custom-call | flops 1073741824 | bytes 2097152 | tf_op jit(solution)/shard_map/pallas_call | solution.py:461
  163.1 3.0 %shard_map.133.refs_4_ = f32[256,2048]{1,0:T(8,128)S(1)} custom-call(bf16[256,256]{1,0:T(8,128)(2,1)S(1)} %shard_map.124.refs_0_, bf16[256,256]{1,0:T(8,128)(2,1)S(1)} %collective-permute-done.14.refs_1_, bf16[512,2048]{1,0:T(8,128)(2,1)} %refs_2_, bf16[512,2048]{1,0:T(8,128)(2,1)} %collective-permute-done.15.refs_6_.refs_3_, f32[256,2048]{1,0:T(8,128)S(1)} %shard_map.132.refs_4_), custom_call_target="tpu_custom_call" | custom-call | flops 536870912 | bytes 2097152 | tf_op jit(solution)/shard_map/pallas_call | solution.py:461
  166.2 5.9 %shard_map.134 = (bf16[256,2048]{1,0:T(8,128)(2,1)}, bf16[64,2048]{1,0:T(8,128)(2,1)}) custom-call(s32[2]{0:T(128)S(1)} %pad_add_fusion.ids, bf16[256,256]{1,0:T(8,128)(2,1)S(1)} %collective-permute-done.10.refs_0_, bf16[256,256]{1,0:T(8,128)(2,1)S(1)} %collective-permute-done.11.refs_1_, bf16[512,2048]{1,0:T(8,128)(2,1)} %collective-permute-done.12.refs_5_.refs_2_, ...), custom_call_target="tpu_custom_call" | custom-call | flops 1073741824 | bytes 8388608 | tf_op jit(solution)/shard_map/pallas_call | solution.py:482
  (60 shorter events, 4.4 us)
Async XLA Ops:
  0.6 16.2 %copy-start = (bf16[1024,512]{1,0:T(8,128)(2,1)S(1)}, bf16[1024,512]{1,0:T(8,128)(2,1)}, u32[]{:S(2)}) copy-start(bf16[1024,512]{1,0:T(8,128)(2,1)} %keys_hbm.3) | copy-start | bytes 3145732
  0.7 1.3 copy-start.3
  2.0 0.7 copy-start.9
  2.7 59.5 %copy-start.10 = (s32[1,256]{1,0:T(1,128)S(1)}, s32[1,256]{1,0:T(1,128)}, u32[]{:S(2)}) copy-start(s32[1,256]{1,0:T(1,128)} %refs_4_.1) | copy-start | bytes 3076
  2.7 59.5 %copy-start.13 = (s32[1,256]{1,0:T(1,128)S(1)}, s32[1,256]{1,0:T(1,128)}, u32[]{:S(2)}) copy-start(s32[1,256]{1,0:T(1,128)} %refs_5_.1) | copy-start | bytes 3076
  3.7 10.1 %collective-permute-start = (bf16[96,2048]{1,0:T(8,128)(2,1)S(1)}, bf16[96,2048]{1,0:T(8,128)(2,1)S(1)}, u32[]{:S(2)}, u32[]{:S(2)}) collective-permute-start(bf16[96,2048]{1,0:T(8,128)(2,1)S(1)} %shard_map.113.refs_0_), channel_id=1, source_target_pairs={{0,2},{1,3},{2,0},{3,1},{4,6},{5,7},{6,4},{7,5},{8,10},{9,11},{10,... | collective-permute-start | bytes 1179656 | tf_op jit(solution)/shard_map/ppermute | solution.py:285
  13.8 1.2 copy-start.7
  13.8 46.0 %collective-permute-start.12 = (bf16[512,2048]{1,0:T(8,128)(2,1)}, bf16[512,2048]{1,0:T(8,128)(2,1)}, u32[]{:S(2)}, u32[]{:S(2)}) collective-permute-start(bf16[512,2048]{1,0:T(8,128)(2,1)} %refs_2_), channel_id=1, source_target_pairs={{0,2},{1,3},{2,0},{3,1},{4,6},{5,7},{6,4},{7,5},{8,10},{9,11},{10,... | collective-permute-start | bytes 6291464 | tf_op jit(solution)/shard_map/ppermute | solution.py:285
  15.0 48.8 %collective-permute-start.1 = (bf16[96,2048]{1,0:T(8,128)(2,1)S(1)}, bf16[96,2048]{1,0:T(8,128)(2,1)}, u32[]{:S(2)}, u32[]{:S(2)}) collective-permute-start(bf16[96,2048]{1,0:T(8,128)(2,1)S(1)} %shard_map.113.refs_0_), channel_id=1, source_target_pairs={{0,1},{1,0},{2,3},{3,2},{4,5},{5,4},{6,7},{7,6},{8,9},{9,8},{10,11... | collective-permute-start | bytes 1179656 | tf_op jit(solution)/shard_map/ppermute | solution.py:285
  16.8 1.2 copy-start.1
  18.2 83.9 %collective-permute-start.16 = (bf16[2048,256]{1,0:T(8,128)(2,1)S(1)}, bf16[2048,256]{1,0:T(8,128)(2,1)S(1)}, u32[]{:S(2)}, u32[]{:S(2)}) collective-permute-start(bf16[2048,256]{1,0:T(8,128)(2,1)S(1)} %shard_map.125.refs_2_.refs_1_), channel_id=1, source_target_pairs={{0,4},{4,0},{8,12},{12,8},{16,20},{20,16},{24,28},{28,24},{1,5},{5... | collective-permute-start | bytes 3145736 | tf_op jit(solution)/shard_map/ppermute | solution.py:335
  18.5 139.9 %collective-permute-start.15 = (bf16[512,2048]{1,0:T(8,128)(2,1)}, bf16[512,2048]{1,0:T(8,128)(2,1)}, u32[]{:S(2)}, u32[]{:S(2)}) collective-permute-start(bf16[512,2048]{1,0:T(8,128)(2,1)} %refs_2_), channel_id=1, source_target_pairs={{0,1},{1,0},{2,3},{3,2},{4,5},{5,4},{6,7},{7,6},{8,9},{9,8},{10,11... | collective-permute-start | bytes 6291464 | tf_op jit(solution)/shard_map/ppermute | solution.py:285
  59.8 98.6 %collective-permute-start.13 = (bf16[512,2048]{1,0:T(8,128)(2,1)}, bf16[512,2048]{1,0:T(8,128)(2,1)}, u32[]{:S(2)}, u32[]{:S(2)}) collective-permute-start(bf16[512,2048]{1,0:T(8,128)(2,1)} %collective-permute-done.12.refs_5_.refs_2_), channel_id=1, source_target_pairs={{0,1},{1,0},{2,3},{3,2},{4,5},{5,4},{6,7},{7,6},{8,9},{9,8},{10,11... | collective-permute-start | bytes 6291464 | tf_op jit(solution)/shard_map/ppermute | solution.py:285
  62.4 4.4 %collective-permute-start.2 = (bf16[96,2048]{1,0:T(8,128)(2,1)}, bf16[96,2048]{1,0:T(8,128)(2,1)S(1)}, u32[]{:S(2)}, u32[]{:S(2)}) collective-permute-start(bf16[96,2048]{1,0:T(8,128)(2,1)} %copy-done.7), channel_id=1, source_target_pairs={{0,1},{1,0},{2,3},{3,2},{4,5},{5,4},{6,7},{7,6},{8,9},{9,8},{10,11... | collective-permute-start | bytes 1179656 | tf_op jit(solution)/shard_map/ppermute | solution.py:285
  62.5 1.2 copy-start.2
  63.7 3.0 %copy-start.5 = (bf16[2048,512]{1,0:T(8,128)(2,1)S(1)}, bf16[2048,512]{1,0:T(8,128)(2,1)}, u32[]{:S(2)}) copy-start(bf16[2048,512]{1,0:T(8,128)(2,1)} %refs_10_.1) | copy-start | bytes 6291460
  63.7 3.0 %copy-start.8 = (bf16[96,2048]{1,0:T(8,128)(2,1)S(1)}, bf16[96,2048]{1,0:T(8,128)(2,1)}, u32[]{:S(2)}) copy-start(bf16[96,2048]{1,0:T(8,128)(2,1)} %copy-done.7) | copy-start | bytes 1179652
  63.7 3.0 %copy-start.11 = (f32[2048]{0:T(1024)S(1)}, f32[2048]{0:T(1024)}, u32[]{:S(2)}) copy-start(f32[2048]{0:T(1024)} %param.15) | copy-start | bytes 24580
  63.7 3.0 %copy-start.12 = (f32[2048]{0:T(1024)S(1)}, f32[2048]{0:T(1024)}, u32[]{:S(2)}) copy-start(f32[2048]{0:T(1024)} %param.16) | copy-start | bytes 24580
  63.8 54.3 %collective-permute-start.3 = (bf16[2048,256]{1,0:T(8,128)(2,1)S(1)}, bf16[2048,256]{1,0:T(8,128)(2,1)S(1)}, u32[]{:S(2)}, u32[]{:S(2)}) collective-permute-start(bf16[2048,256]{1,0:T(8,128)(2,1)S(1)} %shard_map.115.refs_2_.refs_1_), channel_id=1, source_target_pairs={{0,4},{4,0},{8,12},{12,8},{16,20},{20,16},{24,28},{28,24},{1,5},{5... | collective-permute-start | bytes 3145736 | tf_op jit(solution)/shard_map/ppermute | solution.py:335
  64.8 38.5 %copy-start.6 = (s32[8,12]{1,0:T(8,128)S(1)}, s32[8,12]{1,0:T(8,128)}, u32[]{:S(2)}) copy-start(s32[8,12]{1,0:T(8,128)} %pattern.25) | copy-start | bytes 1156
  71.0 6.6 %collective-permute-start.8 = (bf16[256,256]{1,0:T(8,128)(2,1)S(1)}, bf16[256,256]{1,0:T(8,128)(2,1)S(1)}, u32[]{:S(2)}, u32[]{:S(2)}) collective-permute-start(bf16[256,256]{1,0:T(8,128)(2,1)S(1)} %get-tuple-element.7.refs_1_), channel_id=1, source_target_pairs={{8,0},{12,4},{16,8},{20,12},{24,16},{28,20},{9,1},{13,5},{17,9},{2... | collective-permute-start | bytes 393224 | tf_op jit(solution)/shard_map/ppermute | solution.py:432
  77.5 10.0 %collective-permute-start.6 = (bf16[256,256]{1,0:T(8,128)(2,1)S(1)}, bf16[256,256]{1,0:T(8,128)(2,1)S(1)}, u32[]{:S(2)}, u32[]{:S(2)}) collective-permute-start(bf16[256,256]{1,0:T(8,128)(2,1)S(1)} %get-tuple-element.7.refs_1_), channel_id=1, source_target_pairs={{16,0},{20,4},{24,8},{28,12},{17,1},{21,5},{25,9},{29,13},{18,2},{... | collective-permute-start | bytes 393224 | tf_op jit(solution)/shard_map/ppermute | solution.py:432
  87.5 5.7 %collective-permute-start.21 = (bf16[256,256]{1,0:T(8,128)(2,1)S(1)}, bf16[256,256]{1,0:T(8,128)(2,1)S(1)}, u32[]{:S(2)}, u32[]{:S(2)}) collective-permute-start(bf16[256,256]{1,0:T(8,128)(2,1)S(1)} %get-tuple-element.9.refs_1_), channel_id=1, source_target_pairs={{8,0},{12,4},{16,8},{20,12},{24,16},{28,20},{9,1},{13,5},{17,9},{2... | collective-permute-start | bytes 393224 | tf_op jit(solution)/shard_map/ppermute | solution.py:432
  93.2 7.5 %collective-permute-start.17 = (bf16[256,256]{1,0:T(8,128)(2,1)S(1)}, bf16[256,256]{1,0:T(8,128)(2,1)S(1)}, u32[]{:S(2)}, u32[]{:S(2)}) collective-permute-start(bf16[256,256]{1,0:T(8,128)(2,1)S(1)} %get-tuple-element.9.refs_1_), channel_id=1, source_target_pairs={{24,0},{28,4},{25,1},{29,5},{26,2},{30,6},{27,3},{31,7}} | collective-permute-start | bytes 393224 | tf_op jit(solution)/shard_map/ppermute | solution.py:432
  100.7 6.6 %collective-permute-start.19 = (bf16[256,256]{1,0:T(8,128)(2,1)S(1)}, bf16[256,256]{1,0:T(8,128)(2,1)S(1)}, u32[]{:S(2)}, u32[]{:S(2)}) collective-permute-start(bf16[256,256]{1,0:T(8,128)(2,1)S(1)} %get-tuple-element.9.refs_1_), channel_id=1, source_target_pairs={{16,0},{20,4},{24,8},{28,12},{17,1},{21,5},{25,9},{29,13},{18,2},{... | collective-permute-start | bytes 393224 | tf_op jit(solution)/shard_map/ppermute | solution.py:432
  102.0 14.8 %collective-permute-start.4 = (bf16[256,256]{1,0:T(8,128)(2,1)S(1)}, bf16[256,256]{1,0:T(8,128)(2,1)S(1)}, u32[]{:S(2)}, u32[]{:S(2)}) collective-permute-start(bf16[256,256]{1,0:T(8,128)(2,1)S(1)} %get-tuple-element.7.refs_1_), channel_id=1, source_target_pairs={{24,0},{28,4},{25,1},{29,5},{26,2},{30,6},{27,3},{31,7}} | collective-permute-start | bytes 393224 | tf_op jit(solution)/shard_map/ppermute | solution.py:432
  107.3 16.4 %collective-permute-start.18 = (bf16[272,256]{1,0:T(8,128)(2,1)S(1)}, bf16[272,256]{1,0:T(8,128)(2,1)S(1)}, u32[]{:S(2)}, u32[]{:S(2)}) collective-permute-start(bf16[272,256]{1,0:T(8,128)(2,1)S(1)} %shard_map.128), channel_id=1, source_target_pairs={{0,24},{4,28},{1,25},{5,29},{2,26},{6,30},{3,27},{7,31}} | collective-permute-start | bytes 417800 | tf_op jit(solution)/shard_map/ppermute | solution.py:441
  116.8 16.5 %collective-permute-start.20 = (bf16[272,256]{1,0:T(8,128)(2,1)S(1)}, bf16[272,256]{1,0:T(8,128)(2,1)S(1)}, u32[]{:S(2)}, u32[]{:S(2)}) collective-permute-start(bf16[272,256]{1,0:T(8,128)(2,1)S(1)} %shard_map.129), channel_id=1, source_target_pairs={{0,16},{4,20},{8,24},{12,28},{1,17},{5,21},{9,25},{13,29},{2,18},{... | collective-permute-start | bytes 417800 | tf_op jit(solution)/shard_map/ppermute | solution.py:441
  118.1 16.5 %collective-permute-start.22 = (bf16[272,256]{1,0:T(8,128)(2,1)S(1)}, bf16[272,256]{1,0:T(8,128)(2,1)S(1)}, u32[]{:S(2)}, u32[]{:S(2)}) collective-permute-start(bf16[272,256]{1,0:T(8,128)(2,1)S(1)} %shard_map.130), channel_id=1, source_target_pairs={{0,8},{4,12},{8,16},{12,20},{16,24},{20,28},{1,9},{5,13},{9,17},{1... | collective-permute-start | bytes 417800 | tf_op jit(solution)/shard_map/ppermute | solution.py:441
  123.8 17.1 %collective-permute-start.5 = (bf16[272,256]{1,0:T(8,128)(2,1)S(1)}, bf16[272,256]{1,0:T(8,128)(2,1)S(1)}, u32[]{:S(2)}, u32[]{:S(2)}) collective-permute-start(bf16[272,256]{1,0:T(8,128)(2,1)S(1)} %shard_map.119), channel_id=1, source_target_pairs={{0,24},{4,28},{1,25},{5,29},{2,26},{6,30},{3,27},{7,31}} | collective-permute-start | bytes 417800 | tf_op jit(solution)/shard_map/ppermute | solution.py:441
  133.3 13.3 %collective-permute-start.7 = (bf16[272,256]{1,0:T(8,128)(2,1)S(1)}, bf16[272,256]{1,0:T(8,128)(2,1)S(1)}, u32[]{:S(2)}, u32[]{:S(2)}) collective-permute-start(bf16[272,256]{1,0:T(8,128)(2,1)S(1)} %shard_map.121), channel_id=1, source_target_pairs={{0,16},{4,20},{8,24},{12,28},{1,17},{5,21},{9,25},{13,29},{2,18},{... | collective-permute-start | bytes 417800 | tf_op jit(solution)/shard_map/ppermute | solution.py:441
  134.7 12.0 %collective-permute-start.9 = (bf16[272,256]{1,0:T(8,128)(2,1)S(1)}, bf16[272,256]{1,0:T(8,128)(2,1)S(1)}, u32[]{:S(2)}, u32[]{:S(2)}) collective-permute-start(bf16[272,256]{1,0:T(8,128)(2,1)S(1)} %shard_map.123), channel_id=1, source_target_pairs={{0,8},{4,12},{8,16},{12,20},{16,24},{20,28},{1,9},{5,13},{9,17},{1... | collective-permute-start | bytes 417800 | tf_op jit(solution)/shard_map/ppermute | solution.py:441
  140.9 13.0 %collective-permute-start.23 = (bf16[256,256]{1,0:T(8,128)(2,1)S(1)}, bf16[256,256]{1,0:T(8,128)(2,1)S(1)}, u32[]{:S(2)}, u32[]{:S(2)}) collective-permute-start(bf16[256,256]{1,0:T(8,128)(2,1)S(1)} %shard_map.131.refs_0_), channel_id=1, source_target_pairs={{0,2},{1,3},{2,0},{3,1},{4,6},{5,7},{6,4},{7,5},{8,10},{9,11},{10,... | collective-permute-start | bytes 393224 | tf_op jit(solution)/shard_map/ppermute | solution.py:285
  147.3 6.5 %collective-permute-start.10 = (bf16[256,256]{1,0:T(8,128)(2,1)S(1)}, bf16[256,256]{1,0:T(8,128)(2,1)S(1)}, u32[]{:S(2)}, u32[]{:S(2)}) collective-permute-start(bf16[256,256]{1,0:T(8,128)(2,1)S(1)} %shard_map.124.refs_0_), channel_id=1, source_target_pairs={{0,2},{1,3},{2,0},{3,1},{4,6},{5,7},{6,4},{7,5},{8,10},{9,11},{10,... | collective-permute-start | bytes 393224 | tf_op jit(solution)/shard_map/ppermute | solution.py:285
  147.7 10.7 %collective-permute-start.24 = (bf16[256,256]{1,0:T(8,128)(2,1)S(1)}, bf16[256,256]{1,0:T(8,128)(2,1)S(1)}, u32[]{:S(2)}, u32[]{:S(2)}) collective-permute-start(bf16[256,256]{1,0:T(8,128)(2,1)S(1)} %shard_map.131.refs_0_), channel_id=1, source_target_pairs={{0,1},{1,0},{2,3},{3,2},{4,5},{5,4},{6,7},{7,6},{8,9},{9,8},{10,11... | collective-permute-start | bytes 393224 | tf_op jit(solution)/shard_map/ppermute | solution.py:285
  153.9 4.5 %collective-permute-start.25 = (bf16[256,256]{1,0:T(8,128)(2,1)S(1)}, bf16[256,256]{1,0:T(8,128)(2,1)S(1)}, u32[]{:S(2)}, u32[]{:S(2)}) collective-permute-start(bf16[256,256]{1,0:T(8,128)(2,1)S(1)} %collective-permute-done.23.refs_1_), channel_id=1, source_target_pairs={{0,1},{1,0},{2,3},{3,2},{4,5},{5,4},{6,7},{7,6},{8,9},{9,8},{10,11... | collective-permute-start | bytes 393224 | tf_op jit(solution)/shard_map/ppermute | solution.py:285
  153.9 9.2 %collective-permute-start.14 = (bf16[256,256]{1,0:T(8,128)(2,1)S(1)}, bf16[256,256]{1,0:T(8,128)(2,1)S(1)}, u32[]{:S(2)}, u32[]{:S(2)}) collective-permute-start(bf16[256,256]{1,0:T(8,128)(2,1)S(1)} %shard_map.124.refs_0_), channel_id=1, source_target_pairs={{0,1},{1,0},{2,3},{3,2},{4,5},{5,4},{6,7},{7,6},{8,9},{9,8},{10,11... | collective-permute-start | bytes 393224 | tf_op jit(solution)/shard_map/ppermute | solution.py:285
  158.3 7.9 %collective-permute-start.11 = (bf16[256,256]{1,0:T(8,128)(2,1)S(1)}, bf16[256,256]{1,0:T(8,128)(2,1)S(1)}, u32[]{:S(2)}, u32[]{:S(2)}) collective-permute-start(bf16[256,256]{1,0:T(8,128)(2,1)S(1)} %collective-permute-done.10.refs_0_), channel_id=1, source_target_pairs={{0,1},{1,0},{2,3},{3,2},{4,5},{5,4},{6,7},{7,6},{8,9},{9,8},{10,11... | collective-permute-start | bytes 393224 | tf_op jit(solution)/shard_map/ppermute | solution.py:285
  163.1 3.1 %copy-start.4 = (bf16[256,2048]{1,0:T(8,128)(2,1)S(1)}, bf16[256,2048]{1,0:T(8,128)(2,1)}, u32[]{:S(2)}) copy-start(bf16[256,2048]{1,0:T(8,128)(2,1)} %refs_8_.1) | copy-start | bytes 3145732

commit v2 on v1

--- a/solution.py
+++ b/solution.py
@@ -3,6 +3,7 @@
 
 import jax
 import jax.numpy as jnp
+import numpy as np
 from jax import lax
 from jax.experimental import pallas as pl
 from jax.experimental.pallas import tpu as pltpu
@@ -68,19 +69,15 @@
     out_ref[...] = contract(one_hot, hidden_ref[...], 1, 0).astype(out_ref.dtype)
 
 
-def query_body(xors, tok, groups, ids, *refs):
+def query_body(xors, tok, ids, *refs):
     count = len(xors)
     pieces = refs[:count]
-    routes_ref, order_ref, gain_ref, router_ref, cos_ref, sin_ref, wq_hbm = refs[count : count + 7]
-    rows_ref, gate_ref = refs[count + 7 : count + 9]
-    query_refs = refs[count + 9 : count + 9 + groups]
-    wq_ref, sem = refs[count + 9 + groups :]
-    load = pltpu.make_async_copy(wq_hbm, wq_ref, sem)
-    load.start()
+    lists_ref, vectors_ref, cos_ref, sin_ref, wq_ref = refs[count : count + 5]
+    rows_ref, gate_ref, query_ref = refs[count + 5 :]
     cap = pieces[0].shape[0]
-    routed = order_ref.shape[1]
-    routes = routes_ref[...]
-    order = order_ref[...]
+    routed = lists_ref.shape[1]
+    routes = lists_ref[0:1, :]
+    order = lists_ref[1:2, :]
     entry = lax.broadcasted_iota(jnp.int32, (cap, routed), 0)
     rows = None
     for xor, piece in zip(xors, pieces):
@@ -91,34 +88,58 @@
         term = contract(one_hot, piece[...], 0, 0)
         rows = term if rows is None else rows + term
     rows_ref[...] = rows.astype(rows_ref.dtype)
-    logit = jnp.sum(rows * router_ref[...], axis=1, keepdims=True)
+    logit = jnp.sum(rows * vectors_ref[1:2, :], axis=1, keepdims=True)
     gate_ref[...] = jnp.broadcast_to(1.0 / (1.0 + jnp.exp(-logit)), gate_ref.shape)
     mean_square = jnp.mean(rows * rows, axis=1, keepdims=True)
-    normed = (rows * lax.rsqrt(mean_square + EPS) * gain_ref[...]).astype(jnp.bfloat16)
-    load.wait()
+    normed = (rows * lax.rsqrt(mean_square + EPS) * vectors_ref[0:1, :]).astype(jnp.bfloat16)
     projected = contract(normed, wq_ref[...], 1, 0)
     cosine = cos_ref[...]
     sine = sin_ref[...]
-    per = query_refs[0].shape[1] // HD
-    for head in range(per * groups):
+    for head in range(query_ref.shape[1] // HD):
         part = projected[:, head * HD : (head + 1) * HD]
         turned = part * cosine + pltpu.roll(part, HD // 2, 1) * sine
-        at = head % per * HD
-        query_refs[head // per][:, at : at + HD] = turned.astype(jnp.bfloat16)
-
-
-def split_body(group, keys_hbm, values_hbm, out_ref, sems):
-    span, width = out_ref.shape[0] // 2, out_ref.shape[1]
-    loads = [
-        pltpu.make_async_copy(
-            source.at[:, pl.ds(group * width, width)],
-            out_ref.at[pl.ds(at * span, span), :],
-            sems.at[at],
-        )
-        for at, source in enumerate((keys_hbm, values_hbm))
-    ]
-    for load in loads:
-        load.start()
+        query_ref[:, head * HD : (head + 1) * HD] = turned.astype(jnp.bfloat16)
+
+
+def angle_body(span, ids, routes_ref, order_ref, gain_ref, router_ref, freq_ref, *out_refs):
+    cos_ref, sin_ref, picked_ref, lists_ref, vectors_ref = out_refs
+    routed = routes_ref.shape[1]
+    routes = routes_ref[...].astype(jnp.float32)
+    entry = lax.broadcasted_iota(jnp.int32, (routed, routed), 0)
+    listed = jnp.transpose(jnp.broadcast_to(routes, (routed, routed)))
+    picked = jnp.sum(jnp.where(order_ref[...] == entry, listed, 0.0), axis=0, keepdims=True)
+    picked_ref[...] = picked.astype(jnp.int32)
+    position = jnp.transpose(jnp.broadcast_to(picked, (HD, routed))) + (ids[0] * span).astype(
+        jnp.float32
+    )
+    angle = position * freq_ref[...]
+    cos_ref[...] = jnp.cos(angle)
+    lane = lax.broadcasted_iota(jnp.int32, angle.shape, 1)
+    sine = jnp.sin(angle)
+    sin_ref[...] = jnp.where(lane < HD // 2, -sine, sine)
+    lists_ref[0:1, :] = routes_ref[...]
+    lists_ref[1:2, :] = order_ref[...]
+    vectors_ref[0:1, :] = gain_ref[...]
+    vectors_ref[1:2, :] = router_ref[...]
+
+
+def copy_body(in_ref, out_ref):
+    out_ref[...] = in_ref[...]
+
+
+def split_body(keys_hbm, values_hbm, *refs):
+    out_refs, sems = refs[:-1], refs[-1]
+    loads = []
+    for group, out_ref in enumerate(out_refs):
+        span, width = out_ref.shape[0] // 2, out_ref.shape[1]
+        for at, source in enumerate((keys_hbm, values_hbm)):
+            load = pltpu.make_async_copy(
+                source.at[:, pl.ds(group * width, width)],
+                out_ref.at[pl.ds(at * span, span), :],
+                sems.at[2 * group + at],
+            )
+            load.start()
+            loads.append(load)
     for load in loads:
         load.wait()
 
@@ -132,7 +153,7 @@
     ]
 
 
-def attend_body(shift, use, prior, n_ctx, ids, pattern, *refs):
+def attend_body(group, shift, use, prior, n_ctx, ids, pattern, *refs):
     masked_own = shift == 0 and "own" in use
     if masked_own:
         qpos_ref, refs = refs[0], refs[1:]
@@ -143,7 +164,7 @@
     out_ref, m_ref, l_ref, acc_ref = refs
     span = spans[0].shape[0] // 2
     chunk = min(span, 1024)
-    heads = q_ref.shape[1] // HD
+    heads = spans[0].shape[1] // HD
     here = ids[0]
     source = here + 2 * shift
     row = jnp.minimum(source, n_ctx - 1)
@@ -158,7 +179,8 @@
         for at in range(0, span, chunk):
             for head in range(heads):
                 cut = slice(head * HD, (head + 1) * HD)
-                scores = contract(kv_ref[at : at + chunk, cut], q_ref[:, cut], 1, 1) * SCALE
+                query = q_ref[:, (group * heads + head) * HD : (group * heads + head + 1) * HD]
+                scores = contract(kv_ref[at : at + chunk, cut], query, 1, 1) * SCALE
                 if masked:
                     kpos = lax.broadcasted_iota(jnp.int32, scores.shape, 0) + at
                     scores = jnp.where(kpos <= qpos_ref[...], scores, NEG)
@@ -317,20 +339,20 @@
     bf16, f32 = jnp.bfloat16, jnp.float32
     shape_of = jax.ShapeDtypeStruct
 
-    held = []
-    for group in range(GROUPS):
-        held.append(
-            run(
-                functools.partial(split_body, group),
-                grid=(1,),
-                scalars=0,
-                in_specs=[in_hbm, in_hbm],
-                out_specs=whole((2 * span, group_width)),
-                out_shape=shape_of((2 * span, group_width), bf16),
-                scratch=[pltpu.SemaphoreType.DMA((2,))],
-                cost=cost_of(0, 8 * span * group_width),
-            )(first_keys, first_values)
-        )
+    held = run(
+        split_body,
+        grid=(1,),
+        scalars=0,
+        in_specs=[in_hbm, in_hbm],
+        out_specs=[whole((2 * span, group_width))] * GROUPS,
+        out_shape=[shape_of((2 * span, group_width), bf16)] * GROUPS,
+        scratch=[pltpu.SemaphoreType.DMA((2 * GROUPS,))],
+        cost=cost_of(0, 8 * span * part),
+        mib=8,
+    )(
+        pltpu.with_memory_space_constraint(first_keys, pltpu.HBM),
+        pltpu.with_memory_space_constraint(first_values, pltpu.HBM),
+    )
     swap = [(c, c ^ 1) for c in range(n_ctx)]
     across = [lax.ppermute(kv, "ctx", swap) for kv in held]
 
@@ -345,53 +367,69 @@
     )(ids, route_list, hidden)
     pieces, xors = gather_pack(outgoing, n_pack)
 
-    picked = jnp.sum(
-        jnp.where(
-            pack_order[0][:, None] == jnp.arange(routed, dtype=jnp.int32)[None, :],
-            route_list[0][None, :],
-            0,
-        ),
-        axis=1,
-    )
-    position = picked + ctx * span
-    half = HD // 2
-    frequency = 10000.0 ** (-jnp.arange(half, dtype=f32) * 2.0 / HD)
-    angle = position.astype(f32)[:, None] * frequency[None, :]
-    cosine, sine = jnp.cos(angle), jnp.sin(angle)
-    cosine = jnp.concatenate([cosine, cosine], axis=1)
-    sine = jnp.concatenate([-sine, sine], axis=1)
-
-    rows, gate, *queries = run(
-        functools.partial(query_body, xors, tok, GROUPS),
+    half = 10000.0 ** (-np.arange(HD // 2, dtype=np.float32) * np.float32(2.0) / np.float32(HD))
+    frequency = np.concatenate([half, half]).astype(np.float32)[None, :]
+    cosine, sine, picked, lists, vectors = run(
+        functools.partial(angle_body, span),
+        grid=(1,),
+        scalars=1,
+        in_specs=[whole((1, routed))] * 2 + [whole((1, width))] * 2 + [whole((1, HD))],
+        out_specs=[whole((routed, HD))] * 2
+        + [whole((1, routed)), whole((2, routed)), whole((2, width))],
+        out_shape=[shape_of((routed, HD), f32)] * 2
+        + [
+            shape_of((1, routed), jnp.int32),
+            shape_of((2, routed), jnp.int32),
+            shape_of((2, width), f32),
+        ],
+        cost=cost_of(100 * routed * HD, 8 * routed * HD),
+        mib=8,
+    )(
+        ids,
+        route_list,
+        pack_order,
+        norm_gain.reshape(1, width),
+        router_weight.reshape(1, width),
+        jnp.asarray(frequency),
+    )
+
+    fetched = run(
+        copy_body,
+        grid=(1,),
+        scalars=0,
+        in_specs=[whole((width, part))],
+        out_specs=whole((width, part)),
+        out_shape=shape_of((width, part), bf16),
+        cost=cost_of(0, 4 * width * part),
+        mib=8,
+    )(w_query)
+
+    rows, gate, queries = run(
+        functools.partial(query_body, xors, tok),
         grid=(1,),
         scalars=1,
         in_specs=[whole((cap, width))] * n_pack
         + [
-            whole((1, routed)),
-            whole((1, routed)),
-            whole((1, width)),
-            whole((1, width)),
+            whole((2, routed)),
+            whole((2, width)),
             whole((routed, HD)),
             whole((routed, HD)),
-            in_hbm,
+            whole((width, part)),
         ],
         out_specs=[whole((routed, width)), whole((routed, HD))]
-        + [whole((routed, group_width))] * GROUPS,
+        + [whole((routed, part))],
         out_shape=[shape_of((routed, width), bf16), shape_of((routed, HD), f32)]
-        + [shape_of((routed, group_width), bf16)] * GROUPS,
-        scratch=[pltpu.VMEM((width, part), bf16), pltpu.SemaphoreType.DMA],
+        + [shape_of((routed, part), bf16)],
         cost=cost_of(2 * routed * width * (part + n_pack * cap), 6 * width * part),
-        mib=32,
+        mib=20,
     )(
         ids,
         *pieces,
-        route_list,
-        pack_order,
-        norm_gain.reshape(1, width),
-        router_weight.reshape(1, width),
+        lists,
+        vectors,
         cosine,
         sine,
-        w_query,
+        fetched,
     )
 
     w_in, _ = lax.optimization_barrier((w_out, pieces[1]))
@@ -399,18 +437,18 @@
 
     def attend(group, shift, query, use, prior=None):
         masked = shift == 0 and "own" in use
-        given = [picked.reshape(1, routed)] if masked else []
+        given = [picked] if masked else []
         specs = [whole((1, routed))] if masked else []
         if prior is not None:
             given.append(prior)
             specs.append(whole((tall, routed)))
         arrays = [held[group] if kind == "own" else across[group] for kind in use]
         return run(
-            functools.partial(attend_body, shift, use, prior is not None, n_ctx),
+            functools.partial(attend_body, group, shift, use, prior is not None, n_ctx),
             grid=(1,),
             scalars=2,
             in_specs=specs
-            + [whole((routed, group_width))]
+            + [whole((routed, part))]
             + [whole((2 * span, group_width))] * len(arrays),
             out_specs=whole((tall, routed)),
             out_shape=shape_of((tall, routed), bf16),
@@ -423,24 +461,24 @@
         )(ids, pattern, *given, query, *arrays)
 
     shifts = list(range(n_ctx // 2 - 1, 0, -1))
+    arrived = {
+        shift: lax.ppermute(queries, "ctx", [(c, c - 2 * shift) for c in range(2 * shift, n_ctx)])
+        for shift in shifts
+    }
     attended = []
     for group in range(GROUPS):
-        query = queries[group]
-        first = attend(group, 0, query, ("own",))
+        first = attend(group, 0, queries, ("own",))
         returned = []
         for shift in shifts:
-            arrived = lax.ppermute(
-                query, "ctx", [(c, c - 2 * shift) for c in range(2 * shift, n_ctx)]
-            )
             if group < GROUPS - 1:
-                partial = attend(group, shift, arrived, ("own", "other"))
+                partial = attend(group, shift, arrived[shift], ("own", "other"))
             else:
-                early = attend(group, shift, arrived, ("own",))
-                partial = attend(group, shift, arrived, ("other",), early)
+                early = attend(group, shift, arrived[shift], ("own",))
+                partial = attend(group, shift, arrived[shift], ("other",), early)
             returned.append(
                 lax.ppermute(partial, "ctx", [(c, c + 2 * shift) for c in range(n_ctx - 2 * shift)])
             )
-        second = attend(group, 0, query, ("other",), first)
+        second = attend(group, 0, queries, ("other",), first)
         attended.append(
             run(
                 functools.partial(merge_body, [0, *shifts]),
@@ -506,7 +544,7 @@
         total,
         rows,
         gate,
-        picked.reshape(1, routed),
+        picked,
         hidden,
     )
     return (hidden_out, packed)

time: 173 us -> 155 us (0.90)
  starting transfers between devices: 36.6 us -> 28.5 us
  Pallas kernels: 52.1 us -> 45.7 us
  local copies, waits for them, and re-layouts: 4.46 us -> 2.57 us
    ppermute x6 -> x3, waiting for transfers between devices: 25.1 us -> 13.1 us  [local(): lax.ppermute(queries, 'ctx', [(c, c - 2 * shift) for c in range(2 * shift...]
    ppermute x2, waiting for transfers between devices: 0.01 us -> 9.07 us  [local(): across = [lax.ppermute(kv, 'ctx', swap) for kv in held]]
    pallas_call x2, Pallas kernels: 7.79 us -> 2.07 us  [project_part(): run(functools.partial(partial_body, count, offset, prior is not None), gr...]
    ppermute x12, starting transfers between devices: 19.3 us -> 14.4 us  [gather_pack(): pieces = pieces + [lax.ppermute(held, 'pack', pairs) for held in pieces]]
    ppermute x6 -> x3, starting transfers between devices: 7.71 us -> 3.85 us  [local(): lax.ppermute(queries, 'ctx', [(c, c - 2 * shift) for c in range(2 * shift...]
    ppermute x12, waiting for transfers between devices: 51.7 us -> 54.7 us  [gather_pack(): pieces = pieces + [lax.ppermute(held, 'pack', pairs) for held in pieces]]
    pallas_call x1, Pallas kernels: 5.89 us -> 3.66 us  [local(): run(functools.partial(finish_body, len(distant), last * group_width), gri...]
    unnamed x28 -> x20, local copies, waits for them, and re-layouts: 4.46 us -> 2.57 us
  transfers between devices with their start and end apart: 26 -> 23, of which waited for: 8 -> 9; matrix products, arithmetic and copies ran while one was open for 1% -> 0% of each run, Pallas kernels for 26% -> 26%
where the time goes in v2:
time: 155 us
  waiting for transfers between devices  76.9 us (50%)
  Pallas kernels  45.7 us (29%)
  starting transfers between devices  28.5 us (18%)
  local copies, waits for them, and re-layouts  2.57 us (2%)
    ppermute x12, waiting for transfers between devices, gather_pack(): pieces = pieces + [lax.ppermute(held, 'pack', pairs) for held in pieces]  54.7 us
    pallas_call x13, Pallas kernels, attend(): run(functools.partial(attend_body, group, shift, use, prior is not None,...  31.9 us
    ppermute x12, starting transfers between devices, gather_pack(): pieces = pieces + [lax.ppermute(held, 'pack', pairs) for held in pieces]  14.4 us
    ppermute x3, waiting for transfers between devices, local(): lax.ppermute(queries, 'ctx', [(c, c - 2 * shift) for c in range(2 * shift...  13.1 us
    ppermute x6, starting transfers between devices, local(): lax.ppermute(partial, 'ctx', [(c, c + 2 * shift) for c in range(n_ctx - 2...  9.67 us
    ppermute x2, waiting for transfers between devices, local(): across = [lax.ppermute(kv, 'ctx', swap) for kv in held]  9.07 us
    ppermute x3, starting transfers between devices, local(): lax.ppermute(queries, 'ctx', [(c, c - 2 * shift) for c in range(2 * shift...  3.85 us
    pallas_call x1, Pallas kernels, local(): run(functools.partial(finish_body, len(distant), last * group_width), gri...  3.66 us
  transfers between devices with their start and end apart: 23, of which 9 were waited for; matrix products, arithmetic and copies ran while one was open for 0% of the time, Pallas kernels for 26%

profile of v2, /device:TPU:5, one launch (start us, length us, event | category | flops | bytes accessed | tf_op | source)
XLA Modules:
  0.0 154.8 jit_solution(5146700604159917658)
XLA Ops:
  0.7 1.2 copy-done.1
  1.9 0.7 copy-done.7
  2.6 1.0 shard_map.123.refs_0_
  3.7 1.3 collective-permute-start
  4.9 8.8 %collective-permute-done.refs_1_ = bf16[96,2048]{1,0:T(8,128)(2,1)S(1)} collective-permute-done((bf16[96,2048]{1,0:T(8,128)(2,1)S(1)}, bf16[96,2048]{1,0:T(8,128)(2,1)S(1)}, u32[]{:S(2)}, u32[]{:S(2)}) %collective-permute-start) | collective-permute-done | bytes 393248 | tf_op jit(solution)/shard_map/ppermute | solution.py:307
  13.7 1.2 collective-permute-start.12
  14.9 1.8 %collective-permute-start.15 = (bf16[512,2048]{1,0:T(8,128)(2,1)}, bf16[512,2048]{1,0:T(8,128)(2,1)S(1)}, u32[]{:S(2)}, u32[]{:S(2)}) collective-permute-start(bf16[512,2048]{1,0:T(8,128)(2,1)} %refs_2_), channel_id=1, source_target_pairs={{0,1},{1,0},{2,3},{3,2},{4,5},{5,4},{6,7},{7,6},{8,9},{9,8},{10,11... | collective-permute-start | bytes 6291464 | tf_op jit(solution)/shard_map/ppermute | solution.py:307
  16.8 42.8 %collective-permute-done.12.refs_5_.refs_2_ = bf16[512,2048]{1,0:T(8,128)(2,1)S(1)} collective-permute-done((bf16[512,2048]{1,0:T(8,128)(2,1)}, bf16[512,2048]{1,0:T(8,128)(2,1)S(1)}, u32[]{:S(2)}, u32[]{:S(2)}) %collective-permute-start.12) | collective-permute-done | bytes 2097184 | tf_op jit(solution)/shard_map/ppermute | solution.py:307
  59.6 2.4 %collective-permute-start.13 = (bf16[512,2048]{1,0:T(8,128)(2,1)S(1)}, bf16[512,2048]{1,0:T(8,128)(2,1)S(1)}, u32[]{:S(2)}, u32[]{:S(2)}) collective-permute-start(bf16[512,2048]{1,0:T(8,128)(2,1)S(1)} %collective-permute-done.12.refs_5_.refs_2_), channel_id=1, source_target_pairs={{0,1},{1,0},{2,3},{3,2},{4,5},{5,4},{6,7},{7,6},{8,9},{9,8},{10,11... | collective-permute-start | bytes 6291464 | tf_op jit(solution)/shard_map/ppermute | solution.py:307
  62.0 1.5 %shard_map.126 = (bf16[2048,256]{1,0:T(8,128)(2,1)S(1)}, bf16[2048,256]{1,0:T(8,128)(2,1)S(1)}) custom-call(bf16[1024,512]{1,0:T(8,128)(2,1)} %keys_hbm.1, bf16[1024,512]{1,0:T(8,128)(2,1)} %values_hbm.1), custom_call_target="tpu_custom_call" | custom-call | bytes 4194304 | tf_op jit(solution)/shard_map/pallas_call | solution.py:342
  63.9 0.8 collective-permute-start.2
  64.6 1.7 %collective-permute-done.1.refs_2_ = bf16[96,2048]{1,0:T(8,128)(2,1)S(1)} collective-permute-done((bf16[96,2048]{1,0:T(8,128)(2,1)S(1)}, bf16[96,2048]{1,0:T(8,128)(2,1)S(1)}, u32[]{:S(2)}, u32[]{:S(2)}) %collective-permute-start.1) | collective-permute-done | bytes 393248 | tf_op jit(solution)/shard_map/ppermute | solution.py:307
  67.0 1.2 shard_map.122
  68.3 2.8 %shard_map.125 = (bf16[256,2048]{1,0:T(8,128)(2,1)S(1)}, f32[256,128]{1,0:T(8,128)S(1)}, bf16[256,512]{1,0:T(8,128)(2,1)S(1)}) custom-call(s32[2]{0:T(128)S(1)} %pad_add_fusion.ids, bf16[96,2048]{1,0:T(8,128)(2,1)S(1)} %shard_map.123.refs_0_, bf16[96,2048]{1,0:T(8,128)(2,1)S(1)} %collective-permute-done.refs_1_, ...), custom_call_target="tpu_custom_call" | custom-call | flops 939524096 | bytes 6291456 | tf_op jit(solution)/shard_map/pallas_call | solution.py:407
  71.1 1.3 collective-permute-start.4
  72.4 9.8 %collective-permute-done.4.refs_0_.refs_1_ = bf16[256,512]{1,0:T(8,128)(2,1)S(1)} collective-permute-done((bf16[256,512]{1,0:T(8,128)(2,1)S(1)}, bf16[256,512]{1,0:T(8,128)(2,1)S(1)}, u32[]{:S(2)}, u32[]{:S(2)}) %collective-permute-start.4) | collective-permute-done | bytes 262176 | tf_op jit(solution)/shard_map/ppermute | solution.py:465
  82.2 1.3 collective-permute-start.6
  83.5 4.3 %collective-permute-done.16.refs_2_ = bf16[2048,256]{1,0:T(8,128)(2,1)S(1)} collective-permute-done((bf16[2048,256]{1,0:T(8,128)(2,1)S(1)}, bf16[2048,256]{1,0:T(8,128)(2,1)S(1)}, u32[]{:S(2)}, u32[]{:S(2)}) %collective-permute-start.16) | collective-permute-done | bytes 1048608 | tf_op jit(solution)/shard_map/ppermute | solution.py:357
  87.8 1.3 collective-permute-start.8
  89.1 3.5 %shard_map.138 = bf16[272,256]{1,0:T(8,128)(2,1)S(1)} custom-call(s32[2]{0:T(128)S(1)} %pad_add_fusion.ids, s32[8,12]{1,0:T(8,128)S(1)} %copy-done.4, bf16[256,512]{1,0:T(8,128)(2,1)S(1)} %collective-permute-done.4.refs_0_.refs_1_, bf16[2048,256]{1,0:T(8,128)(2,1)S(1)} %get-tuple-element.21.refs_2_.refs_1_, bf16[2048,256]{1,0:T(8,128)(2,1)S(1)} %collective-permute-done.16.refs_2_), custom_call_target="tpu_custom_call" | custom-call | flops 536870912 | bytes 1048576 | tf_op jit(solution)/shard_map/pallas_call | solution.py:446
  92.6 2.6 %collective-permute-done.6.refs_0_.refs_1_ = bf16[256,512]{1,0:T(8,128)(2,1)S(1)} collective-permute-done((bf16[256,512]{1,0:T(8,128)(2,1)S(1)}, bf16[256,512]{1,0:T(8,128)(2,1)S(1)}, u32[]{:S(2)}, u32[]{:S(2)}) %collective-permute-start.6) | collective-permute-done | bytes 262176 | tf_op jit(solution)/shard_map/ppermute | solution.py:465
  95.2 1.3 collective-permute-start.17
  96.5 3.5 %shard_map.139 = bf16[272,256]{1,0:T(8,128)(2,1)S(1)} custom-call(s32[2]{0:T(128)S(1)} %pad_add_fusion.ids, s32[8,12]{1,0:T(8,128)S(1)} %copy-done.4, bf16[256,512]{1,0:T(8,128)(2,1)S(1)} %collective-permute-done.6.refs_0_.refs_1_, bf16[2048,256]{1,0:T(8,128)(2,1)S(1)} %get-tuple-element.21.refs_2_.refs_1_, bf16[2048,256]{1,0:T(8,128)(2,1)S(1)} %collective-permute-done.16.refs_2_), custom_call_target="tpu_custom_call" | custom-call | flops 536870912 | bytes 1048576 | tf_op jit(solution)/shard_map/pallas_call | solution.py:446
  100.0 0.8 collective-permute-done.8.refs_0_.refs_1_
  100.7 1.3 collective-permute-start.18
  102.0 3.5 %shard_map.140 = bf16[272,256]{1,0:T(8,128)(2,1)S(1)} custom-call(s32[2]{0:T(128)S(1)} %pad_add_fusion.ids, s32[8,12]{1,0:T(8,128)S(1)} %copy-done.4, bf16[256,512]{1,0:T(8,128)(2,1)S(1)} %collective-permute-done.8.refs_0_.refs_1_, bf16[2048,256]{1,0:T(8,128)(2,1)S(1)} %get-tuple-element.21.refs_2_.refs_1_, bf16[2048,256]{1,0:T(8,128)(2,1)S(1)} %collective-permute-done.16.refs_2_), custom_call_target="tpu_custom_call" | custom-call | flops 536870912 | bytes 1048576 | tf_op jit(solution)/shard_map/pallas_call | solution.py:446
  105.5 4.8 %collective-permute-done.3.refs_2_ = bf16[2048,256]{1,0:T(8,128)(2,1)S(1)} collective-permute-done((bf16[2048,256]{1,0:T(8,128)(2,1)S(1)}, bf16[2048,256]{1,0:T(8,128)(2,1)S(1)}, u32[]{:S(2)}, u32[]{:S(2)}) %collective-permute-start.3) | collective-permute-done | bytes 1048608 | tf_op jit(solution)/shard_map/ppermute | solution.py:357
  110.3 3.2 %collective-permute-start.19 = (bf16[272,256]{1,0:T(8,128)(2,1)S(1)}, bf16[272,256]{1,0:T(8,128)(2,1)S(1)}, u32[]{:S(2)}, u32[]{:S(2)}) collective-permute-start(bf16[272,256]{1,0:T(8,128)(2,1)S(1)} %shard_map.140), channel_id=1, source_target_pairs={{0,8},{4,12},{8,16},{12,20},{16,24},{20,28},{1,9},{5,13},{9,17},{1... | collective-permute-start | bytes 417800 | tf_op jit(solution)/shard_map/ppermute | solution.py:479
  113.5 2.1 %shard_map.129.refs_0_ = bf16[272,256]{1,0:T(8,128)(2,1)S(1)} custom-call(s32[2]{0:T(128)S(1)} %pad_add_fusion.ids, s32[8,12]{1,0:T(8,128)S(1)} %copy-done.4, bf16[256,512]{1,0:T(8,128)(2,1)S(1)} %collective-permute-done.4.refs_0_.refs_1_, bf16[2048,256]{1,0:T(8,128)(2,1)S(1)} %get-tuple-element.19.refs_2_.refs_1_), custom_call_target="tpu_custom_call" | custom-call | flops 268435456 | bytes 1048576 | tf_op jit(solution)/shard_map/pallas_call | solution.py:446
  115.6 2.3 %shard_map.130 = bf16[272,256]{1,0:T(8,128)(2,1)S(1)} custom-call(s32[2]{0:T(128)S(1)} %pad_add_fusion.ids, s32[8,12]{1,0:T(8,128)S(1)} %copy-done.4, bf16[272,256]{1,0:T(8,128)(2,1)S(1)} %shard_map.129.refs_0_, bf16[256,512]{1,0:T(8,128)(2,1)S(1)} %collective-permute-done.4.refs_0_.refs_1_, bf16[2048,256]{1,0:T(8,128)(2,1)S(1)} %collective-permute-done.3.refs_2_), custom_call_target="tpu_custom_call" | custom-call | flops 268435456 | bytes 1048576 | tf_op jit(solution)/shard_map/pallas_call | solution.py:446
  117.8 1.3 collective-permute-start.5
  119.1 2.1 %shard_map.133.refs_0_ = bf16[272,256]{1,0:T(8,128)(2,1)S(1)} custom-call(s32[2]{0:T(128)S(1)} %pad_add_fusion.ids, s32[8,12]{1,0:T(8,128)S(1)} %copy-done.4, bf16[256,512]{1,0:T(8,128)(2,1)S(1)} %collective-permute-done.8.refs_0_.refs_1_, bf16[2048,256]{1,0:T(8,128)(2,1)S(1)} %get-tuple-element.19.refs_2_.refs_1_), custom_call_target="tpu_custom_call" | custom-call | flops 268435456 | bytes 1048576 | tf_op jit(solution)/shard_map/pallas_call | solution.py:446
  121.2 2.1 %shard_map.131.refs_0_ = bf16[272,256]{1,0:T(8,128)(2,1)S(1)} custom-call(s32[2]{0:T(128)S(1)} %pad_add_fusion.ids, s32[8,12]{1,0:T(8,128)S(1)} %copy-done.4, bf16[256,512]{1,0:T(8,128)(2,1)S(1)} %collective-permute-done.6.refs_0_.refs_1_, bf16[2048,256]{1,0:T(8,128)(2,1)S(1)} %get-tuple-element.19.refs_2_.refs_1_), custom_call_target="tpu_custom_call" | custom-call | flops 268435456 | bytes 1048576 | tf_op jit(solution)/shard_map/pallas_call | solution.py:446
  123.3 2.1 %shard_map.134 = bf16[272,256]{1,0:T(8,128)(2,1)S(1)} custom-call(s32[2]{0:T(128)S(1)} %pad_add_fusion.ids, s32[8,12]{1,0:T(8,128)S(1)} %copy-done.4, bf16[272,256]{1,0:T(8,128)(2,1)S(1)} %shard_map.133.refs_0_, bf16[256,512]{1,0:T(8,128)(2,1)S(1)} %collective-permute-done.8.refs_0_.refs_1_, bf16[2048,256]{1,0:T(8,128)(2,1)S(1)} %collective-permute-done.3.refs_2_), custom_call_target="tpu_custom_call" | custom-call | flops 268435456 | bytes 1048576 | tf_op jit(solution)/shard_map/pallas_call | solution.py:446
  125.4 2.1 %shard_map.132 = bf16[272,256]{1,0:T(8,128)(2,1)S(1)} custom-call(s32[2]{0:T(128)S(1)} %pad_add_fusion.ids, s32[8,12]{1,0:T(8,128)S(1)} %copy-done.4, bf16[272,256]{1,0:T(8,128)(2,1)S(1)} %shard_map.131.refs_0_, bf16[256,512]{1,0:T(8,128)(2,1)S(1)} %collective-permute-done.6.refs_0_.refs_1_, bf16[2048,256]{1,0:T(8,128)(2,1)S(1)} %collective-permute-done.3.refs_2_), custom_call_target="tpu_custom_call" | custom-call | flops 268435456 | bytes 1048576 | tf_op jit(solution)/shard_map/pallas_call | solution.py:446
  127.5 1.3 collective-permute-start.7
  128.8 1.3 collective-permute-start.9
  130.1 2.2 %shard_map.136.refs_0_ = bf16[272,256]{1,0:T(8,128)(2,1)S(1)} custom-call(s32[2]{0:T(128)S(1)} %pad_add_fusion.ids, s32[8,12]{1,0:T(8,128)S(1)} %copy-done.4, s32[1,256]{1,0:T(1,128)S(1)} %get-tuple-element.13.refs_0_.refs_7_, bf16[256,512]{1,0:T(8,128)(2,1)S(1)} %get-tuple-element.18.refs_1_, bf16[2048,256]{1,0:T(8,128)(2,1)S(1)} %get-tuple-element.21.refs_2_.refs_1_), custom_call_target="tpu_custom_call" | custom-call | flops 268435456 | bytes 1048576 | tf_op jit(solution)/shard_map/pallas_call | solution.py:446
  132.3 2.1 %shard_map.137.refs_0_ = bf16[272,256]{1,0:T(8,128)(2,1)S(1)} custom-call(s32[2]{0:T(128)S(1)} %pad_add_fusion.ids, s32[8,12]{1,0:T(8,128)S(1)} %copy-done.4, bf16[272,256]{1,0:T(8,128)(2,1)S(1)} %shard_map.136.refs_0_, bf16[256,512]{1,0:T(8,128)(2,1)S(1)} %get-tuple-element.18.refs_1_, bf16[2048,256]{1,0:T(8,128)(2,1)S(1)} %collective-permute-done.16.refs_2_), custom_call_target="tpu_custom_call" | custom-call | flops 268435456 | bytes 1048576 | tf_op jit(solution)/shard_map/pallas_call | solution.py:446
  135.1 1.3 collective-permute-start.20
  136.4 2.2 %shard_map.127.refs_0_ = bf16[272,256]{1,0:T(8,128)(2,1)S(1)} custom-call(s32[2]{0:T(128)S(1)} %pad_add_fusion.ids, s32[8,12]{1,0:T(8,128)S(1)} %copy-done.4, s32[1,256]{1,0:T(1,128)S(1)} %get-tuple-element.13.refs_0_.refs_7_, bf16[256,512]{1,0:T(8,128)(2,1)S(1)} %get-tuple-element.18.refs_1_, bf16[2048,256]{1,0:T(8,128)(2,1)S(1)} %get-tuple-element.19.refs_2_.refs_1_), custom_call_target="tpu_custom_call" | custom-call | flops 268435456 | bytes 1048576 | tf_op jit(solution)/shard_map/pallas_call | solution.py:446
  138.6 2.3 %shard_map.128.refs_0_ = bf16[272,256]{1,0:T(8,128)(2,1)S(1)} custom-call(s32[2]{0:T(128)S(1)} %pad_add_fusion.ids, s32[8,12]{1,0:T(8,128)S(1)} %copy-done.4, bf16[272,256]{1,0:T(8,128)(2,1)S(1)} %shard_map.127.refs_0_, bf16[256,512]{1,0:T(8,128)(2,1)S(1)} %get-tuple-element.18.refs_1_, bf16[2048,256]{1,0:T(8,128)(2,1)S(1)} %collective-permute-done.3.refs_2_), custom_call_target="tpu_custom_call" | custom-call | flops 268435456 | bytes 1048576 | tf_op jit(solution)/shard_map/pallas_call | solution.py:446
  141.9 2.2 %collective-permute-start.21 = (bf16[256,256]{1,0:T(8,128)(2,1)S(1)}, bf16[256,256]{1,0:T(8,128)(2,1)S(1)}, u32[]{:S(2)}, u32[]{:S(2)}) collective-permute-start(bf16[256,256]{1,0:T(8,128)(2,1)S(1)} %shard_map.141.refs_0_), channel_id=1, source_target_pairs={{0,1},{1,0},{2,3},{3,2},{4,5},{5,4},{6,7},{7,6},{8,9},{9,8},{10,11... | collective-permute-start | bytes 393224 | tf_op jit(solution)/shard_map/ppermute | solution.py:307
  144.1 1.3 collective-permute-done.10.refs_0_
  145.5 3.1 %collective-permute-start.14 = (bf16[256,256]{1,0:T(8,128)(2,1)S(1)}, bf16[256,256]{1,0:T(8,128)(2,1)S(1)}, u32[]{:S(2)}, u32[]{:S(2)}) collective-permute-start(bf16[256,256]{1,0:T(8,128)(2,1)S(1)} %shard_map.135.refs_0_), channel_id=1, source_target_pairs={{0,1},{1,0},{2,3},{3,2},{4,5},{5,4},{6,7},{7,6},{8,9},{9,8},{10,11... | collective-permute-start | bytes 393224 | tf_op jit(solution)/shard_map/ppermute | solution.py:307
  148.6 1.3 shard_map.142.refs_4_
  149.9 0.8 shard_map.143.refs_4_
  151.1 3.7 %shard_map.144 = (bf16[256,2048]{1,0:T(8,128)(2,1)}, bf16[64,2048]{1,0:T(8,128)(2,1)}) custom-call(s32[2]{0:T(128)S(1)} %pad_add_fusion.ids, bf16[256,256]{1,0:T(8,128)(2,1)S(1)} %collective-permute-done.10.refs_0_, bf16[256,256]{1,0:T(8,128)(2,1)S(1)} %collective-permute-done.11.refs_1_, bf16[512,2048]{1,0:T(8,128)(2,1)S(1)} %collective-permute-done.12.refs_5_.refs_2_, ...), custom_call_target="tpu_custom_call" | custom-call | flops 1073741824 | bytes 8388608 | tf_op jit(solution)/shard_map/pallas_call | solution.py:520
  (42 shorter events, 3.2 us)
Async XLA Ops:
  0.7 1.2 copy-start.1
  1.9 0.7 copy-start.7
  2.6 64.0 %copy-start.3 = (bf16[2048,512]{1,0:T(8,128)(2,1)S(1)}, bf16[2048,512]{1,0:T(8,128)(2,1)}, u32[]{:S(2)}) copy-start(bf16[2048,512]{1,0:T(8,128)(2,1)} %in_ref.1) | copy-start | bytes 6291460
  3.7 10.1 %collective-permute-start = (bf16[96,2048]{1,0:T(8,128)(2,1)S(1)}, bf16[96,2048]{1,0:T(8,128)(2,1)S(1)}, u32[]{:S(2)}, u32[]{:S(2)}) collective-permute-start(bf16[96,2048]{1,0:T(8,128)(2,1)S(1)} %shard_map.123.refs_0_), channel_id=1, source_target_pairs={{0,2},{1,3},{2,0},{3,1},{4,6},{5,7},{6,4},{7,5},{8,10},{9,11},{10,... | collective-permute-start | bytes 1179656 | tf_op jit(solution)/shard_map/ppermute | solution.py:307
  13.7 45.9 %collective-permute-start.12 = (bf16[512,2048]{1,0:T(8,128)(2,1)}, bf16[512,2048]{1,0:T(8,128)(2,1)S(1)}, u32[]{:S(2)}, u32[]{:S(2)}) collective-permute-start(bf16[512,2048]{1,0:T(8,128)(2,1)} %refs_2_), channel_id=1, source_target_pairs={{0,2},{1,3},{2,0},{3,1},{4,6},{5,7},{6,4},{7,5},{8,10},{9,11},{10,... | collective-permute-start | bytes 6291464 | tf_op jit(solution)/shard_map/ppermute | solution.py:307
  14.9 133.6 %collective-permute-start.15 = (bf16[512,2048]{1,0:T(8,128)(2,1)}, bf16[512,2048]{1,0:T(8,128)(2,1)S(1)}, u32[]{:S(2)}, u32[]{:S(2)}) collective-permute-start(bf16[512,2048]{1,0:T(8,128)(2,1)} %refs_2_), channel_id=1, source_target_pairs={{0,1},{1,0},{2,3},{3,2},{4,5},{5,4},{6,7},{7,6},{8,9},{9,8},{10,11... | collective-permute-start | bytes 6291464 | tf_op jit(solution)/shard_map/ppermute | solution.py:307
  59.6 89.0 %collective-permute-start.13 = (bf16[512,2048]{1,0:T(8,128)(2,1)S(1)}, bf16[512,2048]{1,0:T(8,128)(2,1)S(1)}, u32[]{:S(2)}, u32[]{:S(2)}) collective-permute-start(bf16[512,2048]{1,0:T(8,128)(2,1)S(1)} %collective-permute-done.12.refs_5_.refs_2_), channel_id=1, source_target_pairs={{0,1},{1,0},{2,3},{3,2},{4,5},{5,4},{6,7},{7,6},{8,9},{9,8},{10,11... | collective-permute-start | bytes 6291464 | tf_op jit(solution)/shard_map/ppermute | solution.py:307
  62.0 4.3 %collective-permute-start.1 = (bf16[96,2048]{1,0:T(8,128)(2,1)S(1)}, bf16[96,2048]{1,0:T(8,128)(2,1)S(1)}, u32[]{:S(2)}, u32[]{:S(2)}) collective-permute-start(bf16[96,2048]{1,0:T(8,128)(2,1)S(1)} %shard_map.123.refs_0_), channel_id=1, source_target_pairs={{0,1},{1,0},{2,3},{3,2},{4,5},{5,4},{6,7},{7,6},{8,9},{9,8},{10,11... | collective-permute-start | bytes 1179656 | tf_op jit(solution)/shard_map/ppermute | solution.py:307
  63.5 24.3 %collective-permute-start.16 = (bf16[2048,256]{1,0:T(8,128)(2,1)S(1)}, bf16[2048,256]{1,0:T(8,128)(2,1)S(1)}, u32[]{:S(2)}, u32[]{:S(2)}) collective-permute-start(bf16[2048,256]{1,0:T(8,128)(2,1)S(1)} %get-tuple-element.21.refs_2_.refs_1_), channel_id=1, source_target_pairs={{0,4},{4,0},{8,12},{12,8},{16,20},{20,16},{24,28},{28,24},{1,5},{5... | collective-permute-start | bytes 3145736 | tf_op jit(solution)/shard_map/ppermute | solution.py:357
  63.9 4.4 %collective-permute-start.2 = (bf16[96,2048]{1,0:T(8,128)(2,1)S(1)}, bf16[96,2048]{1,0:T(8,128)(2,1)S(1)}, u32[]{:S(2)}, u32[]{:S(2)}) collective-permute-start(bf16[96,2048]{1,0:T(8,128)(2,1)S(1)} %collective-permute-done.refs_1_), channel_id=1, source_target_pairs={{0,1},{1,0},{2,3},{3,2},{4,5},{5,4},{6,7},{7,6},{8,9},{9,8},{10,11... | collective-permute-start | bytes 1179656 | tf_op jit(solution)/shard_map/ppermute | solution.py:307
  66.3 0.7 copy-start.5
  66.3 0.7 copy-start.6
  66.3 0.7 copy-start.8
  66.3 0.7 copy-start.9
  66.3 43.9 %collective-permute-start.3 = (bf16[2048,256]{1,0:T(8,128)(2,1)S(1)}, bf16[2048,256]{1,0:T(8,128)(2,1)S(1)}, u32[]{:S(2)}, u32[]{:S(2)}) collective-permute-start(bf16[2048,256]{1,0:T(8,128)(2,1)S(1)} %get-tuple-element.19.refs_2_.refs_1_), channel_id=1, source_target_pairs={{0,4},{4,0},{8,12},{12,8},{16,20},{20,16},{24,28},{28,24},{1,5},{5... | collective-permute-start | bytes 3145736 | tf_op jit(solution)/shard_map/ppermute | solution.py:357
  66.8 22.3 %copy-start.4 = (s32[8,12]{1,0:T(8,128)S(1)}, s32[8,12]{1,0:T(8,128)}, u32[]{:S(2)}) copy-start(s32[8,12]{1,0:T(8,128)} %pattern.25) | copy-start | bytes 1156
  71.1 11.1 %collective-permute-start.4 = (bf16[256,512]{1,0:T(8,128)(2,1)S(1)}, bf16[256,512]{1,0:T(8,128)(2,1)S(1)}, u32[]{:S(2)}, u32[]{:S(2)}) collective-permute-start(bf16[256,512]{1,0:T(8,128)(2,1)S(1)} %get-tuple-element.18.refs_1_), channel_id=1, source_target_pairs={{24,0},{28,4},{25,1},{29,5},{26,2},{30,6},{27,3},{31,7}} | collective-permute-start | bytes 786440 | tf_op jit(solution)/shard_map/ppermute | solution.py:465
  82.2 13.0 %collective-permute-start.6 = (bf16[256,512]{1,0:T(8,128)(2,1)S(1)}, bf16[256,512]{1,0:T(8,128)(2,1)S(1)}, u32[]{:S(2)}, u32[]{:S(2)}) collective-permute-start(bf16[256,512]{1,0:T(8,128)(2,1)S(1)} %get-tuple-element.18.refs_1_), channel_id=1, source_target_pairs={{16,0},{20,4},{24,8},{28,12},{17,1},{21,5},{25,9},{29,13},{18,2},{... | collective-permute-start | bytes 786440 | tf_op jit(solution)/shard_map/ppermute | solution.py:465
  87.8 12.9 %collective-permute-start.8 = (bf16[256,512]{1,0:T(8,128)(2,1)S(1)}, bf16[256,512]{1,0:T(8,128)(2,1)S(1)}, u32[]{:S(2)}, u32[]{:S(2)}) collective-permute-start(bf16[256,512]{1,0:T(8,128)(2,1)S(1)} %get-tuple-element.18.refs_1_), channel_id=1, source_target_pairs={{8,0},{12,4},{16,8},{20,12},{24,16},{28,20},{9,1},{13,5},{17,9},{2... | collective-permute-start | bytes 786440 | tf_op jit(solution)/shard_map/ppermute | solution.py:465
  95.2 22.7 %collective-permute-start.17 = (bf16[272,256]{1,0:T(8,128)(2,1)S(1)}, bf16[272,256]{1,0:T(8,128)(2,1)S(1)}, u32[]{:S(2)}, u32[]{:S(2)}) collective-permute-start(bf16[272,256]{1,0:T(8,128)(2,1)S(1)} %shard_map.138), channel_id=1, source_target_pairs={{0,24},{4,28},{1,25},{5,29},{2,26},{6,30},{3,27},{7,31}} | collective-permute-start | bytes 417800 | tf_op jit(solution)/shard_map/ppermute | solution.py:479
  100.7 26.7 %collective-permute-start.18 = (bf16[272,256]{1,0:T(8,128)(2,1)S(1)}, bf16[272,256]{1,0:T(8,128)(2,1)S(1)}, u32[]{:S(2)}, u32[]{:S(2)}) collective-permute-start(bf16[272,256]{1,0:T(8,128)(2,1)S(1)} %shard_map.139), channel_id=1, source_target_pairs={{0,16},{4,20},{8,24},{12,28},{1,17},{5,21},{9,25},{13,29},{2,18},{... | collective-permute-start | bytes 417800 | tf_op jit(solution)/shard_map/ppermute | solution.py:479
  110.3 18.5 %collective-permute-start.19 = (bf16[272,256]{1,0:T(8,128)(2,1)S(1)}, bf16[272,256]{1,0:T(8,128)(2,1)S(1)}, u32[]{:S(2)}, u32[]{:S(2)}) collective-permute-start(bf16[272,256]{1,0:T(8,128)(2,1)S(1)} %shard_map.140), channel_id=1, source_target_pairs={{0,8},{4,12},{8,16},{12,20},{16,24},{20,28},{1,9},{5,13},{9,17},{1... | collective-permute-start | bytes 417800 | tf_op jit(solution)/shard_map/ppermute | solution.py:479
  117.8 17.2 %collective-permute-start.5 = (bf16[272,256]{1,0:T(8,128)(2,1)S(1)}, bf16[272,256]{1,0:T(8,128)(2,1)S(1)}, u32[]{:S(2)}, u32[]{:S(2)}) collective-permute-start(bf16[272,256]{1,0:T(8,128)(2,1)S(1)} %shard_map.130), channel_id=1, source_target_pairs={{0,24},{4,28},{1,25},{5,29},{2,26},{6,30},{3,27},{7,31}} | collective-permute-start | bytes 417800 | tf_op jit(solution)/shard_map/ppermute | solution.py:479
  127.5 13.4 %collective-permute-start.7 = (bf16[272,256]{1,0:T(8,128)(2,1)S(1)}, bf16[272,256]{1,0:T(8,128)(2,1)S(1)}, u32[]{:S(2)}, u32[]{:S(2)}) collective-permute-start(bf16[272,256]{1,0:T(8,128)(2,1)S(1)} %shard_map.132), channel_id=1, source_target_pairs={{0,16},{4,20},{8,24},{12,28},{1,17},{5,21},{9,25},{13,29},{2,18},{... | collective-permute-start | bytes 417800 | tf_op jit(solution)/shard_map/ppermute | solution.py:479
  128.8 12.1 %collective-permute-start.9 = (bf16[272,256]{1,0:T(8,128)(2,1)S(1)}, bf16[272,256]{1,0:T(8,128)(2,1)S(1)}, u32[]{:S(2)}, u32[]{:S(2)}) collective-permute-start(bf16[272,256]{1,0:T(8,128)(2,1)S(1)} %shard_map.134), channel_id=1, source_target_pairs={{0,8},{4,12},{8,16},{12,20},{16,24},{20,28},{1,9},{5,13},{9,17},{1... | collective-permute-start | bytes 417800 | tf_op jit(solution)/shard_map/ppermute | solution.py:479
  134.4 14.2 %copy-start = (bf16[512,2048]{1,0:T(8,128)(2,1)S(1)}, bf16[512,2048]{1,0:T(8,128)(2,1)}, u32[]{:S(2)}) copy-start(bf16[512,2048]{1,0:T(8,128)(2,1)} %refs_2_) | copy-start | bytes 6291460
  135.1 9.0 %collective-permute-start.20 = (bf16[256,256]{1,0:T(8,128)(2,1)S(1)}, bf16[256,256]{1,0:T(8,128)(2,1)S(1)}, u32[]{:S(2)}, u32[]{:S(2)}) collective-permute-start(bf16[256,256]{1,0:T(8,128)(2,1)S(1)} %shard_map.141.refs_0_), channel_id=1, source_target_pairs={{0,2},{1,3},{2,0},{3,1},{4,6},{5,7},{6,4},{7,5},{8,10},{9,11},{10,... | collective-permute-start | bytes 393224 | tf_op jit(solution)/shard_map/ppermute | solution.py:307
  141.6 3.9 %collective-permute-start.10 = (bf16[256,256]{1,0:T(8,128)(2,1)S(1)}, bf16[256,256]{1,0:T(8,128)(2,1)S(1)}, u32[]{:S(2)}, u32[]{:S(2)}) collective-permute-start(bf16[256,256]{1,0:T(8,128)(2,1)S(1)} %shard_map.135.refs_0_), channel_id=1, source_target_pairs={{0,2},{1,3},{2,0},{3,1},{4,6},{5,7},{6,4},{7,5},{8,10},{9,11},{10,... | collective-permute-start | bytes 393224 | tf_op jit(solution)/shard_map/ppermute | solution.py:307
  141.9 6.6 %collective-permute-start.21 = (bf16[256,256]{1,0:T(8,128)(2,1)S(1)}, bf16[256,256]{1,0:T(8,128)(2,1)S(1)}, u32[]{:S(2)}, u32[]{:S(2)}) collective-permute-start(bf16[256,256]{1,0:T(8,128)(2,1)S(1)} %shard_map.141.refs_0_), channel_id=1, source_target_pairs={{0,1},{1,0},{2,3},{3,2},{4,5},{5,4},{6,7},{7,6},{8,9},{9,8},{10,11... | collective-permute-start | bytes 393224 | tf_op jit(solution)/shard_map/ppermute | solution.py:307
  144.1 4.4 %collective-permute-start.22 = (bf16[256,256]{1,0:T(8,128)(2,1)S(1)}, bf16[256,256]{1,0:T(8,128)(2,1)S(1)}, u32[]{:S(2)}, u32[]{:S(2)}) collective-permute-start(bf16[256,256]{1,0:T(8,128)(2,1)S(1)} %collective-permute-done.20.refs_1_), channel_id=1, source_target_pairs={{0,1},{1,0},{2,3},{3,2},{4,5},{5,4},{6,7},{7,6},{8,9},{9,8},{10,11... | collective-permute-start | bytes 393224 | tf_op jit(solution)/shard_map/ppermute | solution.py:307
  145.5 4.4 %collective-permute-start.14 = (bf16[256,256]{1,0:T(8,128)(2,1)S(1)}, bf16[256,256]{1,0:T(8,128)(2,1)S(1)}, u32[]{:S(2)}, u32[]{:S(2)}) collective-permute-start(bf16[256,256]{1,0:T(8,128)(2,1)S(1)} %shard_map.135.refs_0_), channel_id=1, source_target_pairs={{0,1},{1,0},{2,3},{3,2},{4,5},{5,4},{6,7},{7,6},{8,9},{9,8},{10,11... | collective-permute-start | bytes 393224 | tf_op jit(solution)/shard_map/ppermute | solution.py:307
  148.5 2.2 %collective-permute-start.11 = (bf16[256,256]{1,0:T(8,128)(2,1)S(1)}, bf16[256,256]{1,0:T(8,128)(2,1)S(1)}, u32[]{:S(2)}, u32[]{:S(2)}) collective-permute-start(bf16[256,256]{1,0:T(8,128)(2,1)S(1)} %collective-permute-done.10.refs_0_), channel_id=1, source_target_pairs={{0,1},{1,0},{2,3},{3,2},{4,5},{5,4},{6,7},{7,6},{8,9},{9,8},{10,11... | collective-permute-start | bytes 393224 | tf_op jit(solution)/shard_map/ppermute | solution.py:307
  149.9 1.2 copy-start.2
